TPU v7x, 32 devices: a whole 2x2x4 slice. The times are simulated.
32 devices in a mesh: gx: 2 (over y), gy: 4 (over x, core), gz: 4 (over z).
Axes of the slice: x: 2, y: 2, z: 4, core: 2. Of those that a mesh axis runs over, the one named last changes fastest.
Arguments:
- displacement: float32 [6, 8, 32, 512], P(None, 'gx', 'gy', 'gz'), may hold values from -6 to 6
- velocity: float32 [6, 8, 32, 512], P(None, 'gx', 'gy', 'gz'), may hold values from -6 to 6
- moments: float32 [6, 8, 32, 512], P(None, 'gx', 'gy', 'gz'), may hold values from -6 to 6
- sector_bit: int32 [2, 8, 32, 512], P(None, 'gx', 'gy', 'gz'), may hold values from 0 to 1
- weight_in: bfloat16 [32, 256], replicated, may hold values from -1 to 1
- bias_in: float32 [256], replicated, may hold values from -3 to 3
- weight_mid: bfloat16 [256, 256], replicated, may hold values from -0.375 to 0.375
- weight_out: bfloat16 [256, 4], replicated, may hold values from -0.375 to 0.375
Outputs:
- displacement_out: float32 [6, 8, 32, 512], P(None, 'gx', 'gy', 'gz')
- velocity_out: float32 [6, 8, 32, 512], P(None, 'gx', 'gy', 'gz')
- moments_out: float32 [6, 8, 32, 512], P(None, 'gx', 'gy', 'gz')
All inputs are finite; a program needn't handle non-finite values.
Results may differ from a plain program's by a relative error of at most 0.0014.
Values sent between devices are 32-bit elements; how exact they have to be, the bound alone decides.
No kernel may reach another device: no remote copies, remote signals or barrier semaphores. Data moves between devices by JAX's collectives and lax.ppermute only.
A program may use at most 64 MiB of HBM per device.

v0:
```python
import jax
import jax.numpy as jnp
from jax import lax
from jax.sharding import PartitionSpec as P

half_step = 0.1
lattice_step = 0.25
second_shell = 0.5


def padded_2(block, sides, width):
    for axis, dim in sides:
        count = lax.axis_size(axis)
        forward = [(i, i + 1) for i in range(count - 1)]
        forward.append((count - 1, 0))
        backward = [(target, source) for source, target in forward]
        low = lax.ppermute(
            lax.slice_in_dim(block, block.shape[dim] - width, None, axis=dim), axis, forward
        )
        high = lax.ppermute(lax.slice_in_dim(block, 0, width, axis=dim), axis, backward)
        block = jnp.concatenate([low, block, high], axis=dim)
    return block


def rotate(moment, field, step):
    square = jnp.sum(field * field, axis=0)
    theta = step * jnp.sqrt(square)
    along = jnp.sinc(theta / jnp.pi)
    across = 0.5 * jnp.sinc(theta / (2.0 * jnp.pi)) ** 2
    cross = jnp.stack(
        [
            field[1] * moment[2] - field[2] * moment[1],
            field[2] * moment[0] - field[0] * moment[2],
            field[0] * moment[1] - field[1] * moment[0],
        ]
    )
    inner = jnp.sum(field * moment, axis=0)
    return jnp.cos(theta) * moment + step * along * cross + step * step * across * inner * field


def features_of(padded, part, sizes):
    size_x, size_y, size_z = sizes
    other = 1 - part
    sign = 2 * part - 1

    def window(first, shift_x, shift_y, shift_z):
        return padded[
            first : first + 3,
            1 + shift_x : 1 + shift_x + size_x,
            1 + shift_y : 1 + shift_y + size_y,
            1 + shift_z : 1 + shift_z + size_z,
        ]

    own_disp = window(3 * part, 0, 0, 0)
    own_spin = window(6 + 3 * part, 0, 0, 0)
    rows = []
    for corner in range(8):
        shift_x = sign * (corner >> 2 & 1)
        shift_y = sign * (corner >> 1 & 1)
        shift_z = sign * (corner & 1)
        near_disp = window(3 * other, shift_x, shift_y, shift_z)
        near_spin = window(6 + 3 * other, shift_x, shift_y, shift_z)
        rows.append(near_disp - own_disp)
        rows.append(jnp.sum(own_spin * near_spin, axis=0, keepdims=True))
    return jnp.concatenate(rows, 0)


def sector_field(spin_pad, coupling_part, part, sizes):
    other = 1 - part
    sign = 2 * part - 1
    block_shape = (3,) + sizes
    near_total = jnp.zeros(block_shape, jnp.float32)
    for corner in range(8):
        start = (
            3 * other,
            1 + sign * (corner >> 2 & 1),
            1 + sign * (corner >> 1 & 1),
            1 + sign * (corner & 1),
        )
        near_total = near_total + lax.dynamic_slice(spin_pad, start, block_shape)
    shell = jnp.zeros(block_shape, jnp.float32)
    for axis_offset in ((1, 0, 0), (-1, 0, 0), (0, 1, 0), (0, -1, 0), (0, 0, 1), (0, 0, -1)):
        start = (3 * part, 1 + axis_offset[0], 1 + axis_offset[1], 1 + axis_offset[2])
        shell = shell + lax.dynamic_slice(spin_pad, start, block_shape)
    return coupling_part[None] * near_total + second_shell * shell


def turn_static(spin_pad, coupling_part, map_part, part, sector, step, sizes):
    size_x, size_y, size_z = sizes
    inner = spin_pad[:, 1 : 1 + size_x, 1 : 1 + size_y, 1 : 1 + size_z]
    own = inner[3 * part : 3 * part + 3]
    field = sector_field(spin_pad, coupling_part, part, sizes)
    turned = rotate(own, field, step)
    updated = jnp.where((map_part == sector)[None], turned, own)
    if part == 0:
        return jnp.concatenate([updated, inner[3:6]], 0)
    return jnp.concatenate([inner[0:3], updated], 0)


def network(block, weight_in, bias_in, weight_mid, weight_out):
    dims = (((0,), (0,)), ((), ()))
    first = lax.dot_general(weight_in, block, dims, preferred_element_type=jnp.float32)
    first = jax.nn.silu(first + bias_in[:, None]).astype(jnp.bfloat16)
    second = lax.dot_general(weight_mid, first, dims, preferred_element_type=jnp.float32)
    second = jax.nn.silu(second).astype(jnp.bfloat16)
    return lax.dot_general(weight_out, second, dims, preferred_element_type=jnp.float32)


def on_device(
    displacement, velocity, moments, sector_bit, weight_in, bias_in, weight_mid, weight_out
):
    size_x, size_y, size_z = (displacement.shape[1], displacement.shape[2], displacement.shape[3])
    sizes = (size_x, size_y, size_z)
    padded = padded_2(
        jnp.concatenate([displacement, moments], 0), (("gx", 1), ("gy", 2), ("gz", 3)), 1
    )
    table_zero = features_of(padded, 0, sizes)
    table_one = features_of(padded, 1, sizes)
    width = table_zero.shape[0]
    inputs = jnp.stack([table_zero, table_one], 1).astype(jnp.bfloat16)
    blocks = inputs.reshape(width, 2 * size_x, size_y * size_z).transpose(1, 0, 2)
    result = lax.map(
        lambda block: network(block, weight_in, bias_in, weight_mid, weight_out), blocks
    )
    heads = result.transpose(1, 0, 2).reshape(4, 2, size_x, size_y, size_z)
    force = jnp.concatenate([heads[0:3, 0], heads[0:3, 1]], 0)
    coupling = 1.0 + 0.5 * jnp.tanh(heads[3])
    velocity_out = velocity + lattice_step * force
    displacement_out = displacement + lattice_step * velocity_out
    index_x = lax.axis_index("gx") * size_x + lax.broadcasted_iota(jnp.int32, sizes, 0)
    index_y = lax.axis_index("gy") * size_y + lax.broadcasted_iota(jnp.int32, sizes, 1)
    index_z = lax.axis_index("gz") * size_z + lax.broadcasted_iota(jnp.int32, sizes, 2)
    parity = (index_x + index_y + index_z) % 2
    sublattice = 4 * jnp.arange(2, dtype=jnp.int32)[:, None, None, None]
    sector_map = sublattice + 2 * sector_bit + parity[None]
    order = list(range(8)) + list(range(7, -1, -1))
    angles = [half_step] * 16
    turns = len(order)
    cycle = padded_2(
        jnp.concatenate([coupling, sector_bit.astype(jnp.float32)], 0),
        (("gx", 1), ("gy", 2), ("gz", 3)),
        1,
    )
    wide = (size_x + 2, size_y + 2, size_z + 2)
    wide_x = lax.axis_index("gx") * size_x - 1 + lax.broadcasted_iota(jnp.int32, wide, 0)
    wide_y = lax.axis_index("gy") * size_y - 1 + lax.broadcasted_iota(jnp.int32, wide, 1)
    wide_z = lax.axis_index("gz") * size_z - 1 + lax.broadcasted_iota(jnp.int32, wide, 2)
    wide_parity = (wide_x + wide_y + wide_z) % 2
    wide_map = sublattice + 2 * cycle[2:4].astype(jnp.int32) + wide_parity[None]
    wide_coupling = cycle[0:2]
    spins = moments
    for first_turn in range(0, turns, 2):
        deep_pad = padded_2(spins, (("gx", 1), ("gy", 2), ("gz", 3)), 2)
        sector = order[first_turn]
        part = sector // 4
        wider = turn_static(
            deep_pad, wide_coupling[part], wide_map[part], part, sector, angles[first_turn], wide
        )
        sector = order[first_turn + 1]
        part = sector // 4
        spins = turn_static(
            wider, coupling[part], sector_map[part], part, sector, angles[first_turn + 1], sizes
        )
    return (displacement_out, velocity_out, spins)


def solution(mesh):
    placed = (
        P(None, "gx", "gy", "gz"),
        P(None, "gx", "gy", "gz"),
        P(None, "gx", "gy", "gz"),
        P(None, "gx", "gy", "gz"),
        P(),
        P(),
        P(),
        P(),
    )
    return jax.shard_map(
        on_device,
        mesh=mesh,
        in_specs=placed,
        out_specs=(P(None, "gx", "gy", "gz"), P(None, "gx", "gy", "gz"), P(None, "gx", "gy", "gz")),
        check_vma=False,
    )
```

profile of v0, /device:TPU:0, one launch (start us, length us, event | category | flops | bytes accessed | tf_op | source)
XLA Modules:
  0.0 290.5 jit_solution(10624043291983227550)
XLA Ops:
  2.5 3.1 %collective-permute-start = (f32[12,1,8,128]{3,2,1,0:T(8,128)S(1)}, f32[12,1,8,128]{3,2,1,0:T(8,128)S(1)}, u32[]{:S(2)}, u32[]{:S(2)}) collective-permute-start(f32[12,1,8,128]{3,2,1,0:T(8,128)S(1)} %get-tuple-element.316), channel_id=1, source_target_pairs={{0,16},{16,0},{1,17},{17,1},{2,18},{18,2},{3,19},{19,3},{4,20},{20... | collective-permute-start | bytes 147464 | tf_op jit(solution)/shard_map/ppermute | solution.py:17
  7.0 1.9 collective-permute-start.6
  15.7 1.7 collective-permute-start.3
  24.8 2.1 collective-permute-done.3
  27.7 1.9 copy-done
  29.6 1.8 collective-permute-start.4
  31.4 2.1 collective-permute-start.5
  38.2 3.1 %copy.381 = f32[12,6,10,128]{3,1,2,0:T(8,128)S(1)} copy(f32[12,6,10,128]{0,3,2,1:T(8,128)} %copy-done) | data formatting | bytes 737280 | tf_op jit(solution)/shard_map/concatenate | solution.py:21
  44.6 8.4 %while.10 = (s32[]{:T(128)}, f32[8,4,1024]{2,1,0:T(4,128)S(1)}, bf16[8,32,1024]{2,1,0:T(8,128)(2,1)S(1)}, bf16[32,256]{1,0:T(8,128)(2,1)S(1)}, f32[256]{0:T(256)...) while((s32[]{:T(128)}, f32[8,4,1024]{2,1,0:T(4,128)S(1)}, ...), condition=%wide.region_16.17_spmd, body=%wide.region_15.0_spmd.sunk | while | flops 155975680 | bytes 1281117 | solution.py:122
  60.6 3.8 %collective-permute-start.17 = (f32[6,8,12,2]{3,1,2,0:T(8,128)S(1)}, f32[6,8,12,2]{3,1,2,0:T(8,128)S(1)}, u32[]{:S(2)}, u32[]{:S(2)}) collective-permute-start(f32[6,8,12,2]{3,1,2,0:T(8,128)S(1)} %get-tuple-element.267), channel_id=1, source_target_pairs={{1,0},{2,1},{3,2},{0,3},{5,4},{6,5},{7,6},{4,7},{9,8},{10,9},{11,1... | collective-permute-start | bytes 13832 | tf_op jit(solution)/shard_map/ppermute | solution.py:20
  64.7 3.8 %collective-permute-start.16 = (f32[4,6,10,1]{3,2,1,0:T(8,128)S(1)}, f32[4,6,10,1]{3,2,1,0:T(8,128)S(1)}, u32[]{:S(2)}, u32[]{:S(2)}) collective-permute-start(f32[4,6,10,1]{3,2,1,0:T(8,128)S(1)} %get-tuple-element.311), channel_id=1, source_target_pairs={{1,0},{2,1},{3,2},{0,3},{5,4},{6,5},{7,6},{4,7},{9,8},{10,9},{11,1... | collective-permute-start | bytes 2888 | tf_op jit(solution)/shard_map/ppermute | solution.py:20
  68.5 3.8 %collective-permute-done.10 = f32[6,8,12,2]{3,1,2,0:T(8,128)S(1)} collective-permute-done((f32[6,8,12,2]{3,1,2,0:T(8,128)S(1)}, f32[6,8,12,2]{3,1,2,0:T(8,128)S(1)}, u32[]{:S(2)}, u32[]{:S(2)}) %collective-permute-start.10) | collective-permute-done | bytes 4640 | tf_op jit(solution)/shard_map/ppermute | solution.py:17
  72.3 5.4 %collective-permute-done.17 = f32[6,8,12,2]{3,1,2,0:T(8,128)S(1)} collective-permute-done((f32[6,8,12,2]{3,1,2,0:T(8,128)S(1)}, f32[6,8,12,2]{3,1,2,0:T(8,128)S(1)}, u32[]{:S(2)}, u32[]{:S(2)}) %collective-permute-start.17) | collective-permute-done | bytes 4640 | tf_op jit(solution)/shard_map/ppermute | solution.py:20
  77.9 4.9 %collective-permute-done.15 = f32[4,6,10,1]{3,2,1,0:T(8,128)S(1)} collective-permute-done((f32[4,6,10,1]{3,2,1,0:T(8,128)S(1)}, f32[4,6,10,1]{3,2,1,0:T(8,128)S(1)}, u32[]{:S(2)}, u32[]{:S(2)}) %collective-permute-start.15) | collective-permute-done | bytes 992 | tf_op jit(solution)/shard_map/ppermute | solution.py:17
  89.4 2.1 collective-permute-done.18
  92.6 1.8 collective-permute-start.21
  96.9 3.2 %collective-permute-start.23 = (f32[6,8,12,2]{3,1,2,0:T(8,128)S(1)}, f32[6,8,12,2]{3,1,2,0:T(8,128)S(1)}, u32[]{:S(2)}, u32[]{:S(2)}) collective-permute-start(f32[6,8,12,2]{3,1,2,0:T(8,128)S(1)} %get-tuple-element.262), channel_id=1, source_target_pairs={{1,0},{2,1},{3,2},{0,3},{5,4},{6,5},{7,6},{4,7},{9,8},{10,9},{11,1... | collective-permute-start | bytes 13832 | tf_op jit(solution)/shard_map/ppermute | solution.py:20
  100.1 7.9 %collective-permute-done.22 = f32[6,8,12,2]{3,1,2,0:T(8,128)S(1)} collective-permute-done((f32[6,8,12,2]{3,1,2,0:T(8,128)S(1)}, f32[6,8,12,2]{3,1,2,0:T(8,128)S(1)}, u32[]{:S(2)}, u32[]{:S(2)}) %collective-permute-start.22) | collective-permute-done | bytes 4640 | tf_op jit(solution)/shard_map/ppermute | solution.py:17
  108.0 5.0 %collective-permute-done.23 = f32[6,8,12,2]{3,1,2,0:T(8,128)S(1)} collective-permute-done((f32[6,8,12,2]{3,1,2,0:T(8,128)S(1)}, f32[6,8,12,2]{3,1,2,0:T(8,128)S(1)}, u32[]{:S(2)}, u32[]{:S(2)}) %collective-permute-start.23) | collective-permute-done | bytes 4640 | tf_op jit(solution)/shard_map/ppermute | solution.py:20
  118.1 2.6 collective-permute-done.25
  121.8 1.8 collective-permute-start.27
  125.5 2.1 collective-permute-start.28
  127.6 7.6 %collective-permute-done.28 = f32[6,8,12,2]{3,1,2,0:T(8,128)S(1)} collective-permute-done((f32[6,8,12,2]{3,1,2,0:T(8,128)S(1)}, f32[6,8,12,2]{3,1,2,0:T(8,128)S(1)}, u32[]{:S(2)}, u32[]{:S(2)}) %collective-permute-start.28) | collective-permute-done | bytes 4640 | tf_op jit(solution)/shard_map/ppermute | solution.py:20
  135.2 7.2 %collective-permute-done.29 = f32[6,8,12,2]{3,1,2,0:T(8,128)S(1)} collective-permute-done((f32[6,8,12,2]{3,1,2,0:T(8,128)S(1)}, f32[6,8,12,2]{3,1,2,0:T(8,128)S(1)}, u32[]{:S(2)}, u32[]{:S(2)}) %collective-permute-start.29) | collective-permute-done | bytes 4640 | tf_op jit(solution)/shard_map/ppermute | solution.py:17
  147.2 2.1 collective-permute-done.31
  150.3 1.8 collective-permute-start.33
  156.1 7.4 %collective-permute-done.34 = f32[6,8,12,2]{3,1,2,0:T(8,128)S(1)} collective-permute-done((f32[6,8,12,2]{3,1,2,0:T(8,128)S(1)}, f32[6,8,12,2]{3,1,2,0:T(8,128)S(1)}, u32[]{:S(2)}, u32[]{:S(2)}) %collective-permute-start.34) | collective-permute-done | bytes 4640 | tf_op jit(solution)/shard_map/ppermute | solution.py:20
  163.5 8.1 %collective-permute-done.35 = f32[6,8,12,2]{3,1,2,0:T(8,128)S(1)} collective-permute-done((f32[6,8,12,2]{3,1,2,0:T(8,128)S(1)}, f32[6,8,12,2]{3,1,2,0:T(8,128)S(1)}, u32[]{:S(2)}, u32[]{:S(2)}) %collective-permute-start.35) | collective-permute-done | bytes 4640 | tf_op jit(solution)/shard_map/ppermute | solution.py:17
  176.4 2.6 collective-permute-done.37
  179.8 1.8 collective-permute-start.39
  183.5 1.8 collective-permute-start.40
  185.5 7.5 %collective-permute-done.40 = f32[6,8,12,2]{3,1,2,0:T(8,128)S(1)} collective-permute-done((f32[6,8,12,2]{3,1,2,0:T(8,128)S(1)}, f32[6,8,12,2]{3,1,2,0:T(8,128)S(1)}, u32[]{:S(2)}, u32[]{:S(2)}) %collective-permute-start.40) | collective-permute-done | bytes 4640 | tf_op jit(solution)/shard_map/ppermute | solution.py:20
  193.0 6.6 %collective-permute-done.41 = f32[6,8,12,2]{3,1,2,0:T(8,128)S(1)} collective-permute-done((f32[6,8,12,2]{3,1,2,0:T(8,128)S(1)}, f32[6,8,12,2]{3,1,2,0:T(8,128)S(1)}, u32[]{:S(2)}, u32[]{:S(2)}) %collective-permute-start.41) | collective-permute-done | bytes 4640 | tf_op jit(solution)/shard_map/ppermute | solution.py:17
  204.5 2.3 collective-permute-done.43
  207.6 1.8 collective-permute-start.45
  211.3 2.1 collective-permute-start.46
  213.4 7.7 %collective-permute-done.46 = f32[6,8,12,2]{3,1,2,0:T(8,128)S(1)} collective-permute-done((f32[6,8,12,2]{3,1,2,0:T(8,128)S(1)}, f32[6,8,12,2]{3,1,2,0:T(8,128)S(1)}, u32[]{:S(2)}, u32[]{:S(2)}) %collective-permute-start.46) | collective-permute-done | bytes 4640 | tf_op jit(solution)/shard_map/ppermute | solution.py:20
  221.1 7.2 %collective-permute-done.47 = f32[6,8,12,2]{3,1,2,0:T(8,128)S(1)} collective-permute-done((f32[6,8,12,2]{3,1,2,0:T(8,128)S(1)}, f32[6,8,12,2]{3,1,2,0:T(8,128)S(1)}, u32[]{:S(2)}, u32[]{:S(2)}) %collective-permute-start.47) | collective-permute-done | bytes 4640 | tf_op jit(solution)/shard_map/ppermute | solution.py:17
  233.0 2.3 collective-permute-done.48
  236.4 1.8 collective-permute-start.51
  241.5 2.5 collective-permute-start.53
  243.9 7.9 %collective-permute-done.52 = f32[6,8,12,2]{3,1,2,0:T(8,128)S(1)} collective-permute-done((f32[6,8,12,2]{3,1,2,0:T(8,128)S(1)}, f32[6,8,12,2]{3,1,2,0:T(8,128)S(1)}, u32[]{:S(2)}, u32[]{:S(2)}) %collective-permute-start.52) | collective-permute-done | bytes 4640 | tf_op jit(solution)/shard_map/ppermute | solution.py:17
  251.8 5.6 %collective-permute-done.53 = f32[6,8,12,2]{3,1,2,0:T(8,128)S(1)} collective-permute-done((f32[6,8,12,2]{3,1,2,0:T(8,128)S(1)}, f32[6,8,12,2]{3,1,2,0:T(8,128)S(1)}, u32[]{:S(2)}, u32[]{:S(2)}) %collective-permute-start.53) | collective-permute-done | bytes 4640 | tf_op jit(solution)/shard_map/ppermute | solution.py:20
  262.6 2.0 collective-permute-done.54
  266.3 1.8 collective-permute-start.57
  271.0 2.9 collective-permute-start.59
  273.9 7.8 %collective-permute-done.58 = f32[6,8,12,2]{3,1,2,0:T(8,128)S(1)} collective-permute-done((f32[6,8,12,2]{3,1,2,0:T(8,128)S(1)}, f32[6,8,12,2]{3,1,2,0:T(8,128)S(1)}, u32[]{:S(2)}, u32[]{:S(2)}) %collective-permute-start.58) | collective-permute-done | bytes 4640 | tf_op jit(solution)/shard_map/ppermute | solution.py:17
  281.7 5.3 %collective-permute-done.59 = f32[6,8,12,2]{3,1,2,0:T(8,128)S(1)} collective-permute-done((f32[6,8,12,2]{3,1,2,0:T(8,128)S(1)}, f32[6,8,12,2]{3,1,2,0:T(8,128)S(1)}, u32[]{:S(2)}, u32[]{:S(2)}) %collective-permute-start.59) | collective-permute-done | bytes 4640 | tf_op jit(solution)/shard_map/ppermute | solution.py:20
  (396 shorter events, 107.2 us)
Async XLA Ops:
  2.5 10.0 %collective-permute-start = (f32[12,1,8,128]{3,2,1,0:T(8,128)S(1)}, f32[12,1,8,128]{3,2,1,0:T(8,128)S(1)}, u32[]{:S(2)}, u32[]{:S(2)}) collective-permute-start(f32[12,1,8,128]{3,2,1,0:T(8,128)S(1)} %get-tuple-element.316), channel_id=1, source_target_pairs={{0,16},{16,0},{1,17},{17,1},{2,18},{18,2},{3,19},{19,3},{4,20},{20... | collective-permute-start | bytes 147464 | tf_op jit(solution)/shard_map/ppermute | solution.py:17
  5.5 6.9 %collective-permute-start.1 = (f32[12,1,8,128]{3,2,1,0:T(8,128)S(1)}, f32[12,1,8,128]{3,2,1,0:T(8,128)S(1)}, u32[]{:S(2)}, u32[]{:S(2)}) collective-permute-start(f32[12,1,8,128]{3,2,1,0:T(8,128)S(1)} %get-tuple-element.317), channel_id=1, source_target_pairs={{16,0},{0,16},{17,1},{1,17},{18,2},{2,18},{19,3},{3,19},{20,4},{4,... | collective-permute-start | bytes 147464 | tf_op jit(solution)/shard_map/ppermute | solution.py:20
  7.0 10.3 %collective-permute-start.6 = (f32[6,2,8,128]{3,2,1,0:T(8,128)}, f32[6,2,8,128]{3,2,1,0:T(8,128)}, u32[]{:S(2)}, u32[]{:S(2)}) collective-permute-start(f32[6,2,8,128]{3,2,1,0:T(8,128)} %get-tuple-element.341), channel_id=1, source_target_pairs={{0,16},{16,0},{1,17},{17,1},{2,18},{18,2},{3,19},{19,3},{4,20},{20... | collective-permute-start | bytes 147464 | tf_op jit(solution)/shard_map/ppermute | solution.py:17
  9.0 8.4 %collective-permute-start.7 = (f32[6,2,8,128]{3,2,1,0:T(8,128)}, f32[6,2,8,128]{3,2,1,0:T(8,128)}, u32[]{:S(2)}, u32[]{:S(2)}) collective-permute-start(f32[6,2,8,128]{3,2,1,0:T(8,128)} %get-tuple-element.342), channel_id=1, source_target_pairs={{16,0},{0,16},{17,1},{1,17},{18,2},{2,18},{19,3},{3,19},{20,4},{4,... | collective-permute-start | bytes 147464 | tf_op jit(solution)/shard_map/ppermute | solution.py:20
  15.6 9.2 %collective-permute-start.2 = (f32[12,6,1,128]{0,3,2,1:T(8,128)S(1)}, f32[12,6,1,128]{0,3,2,1:T(8,128)S(1)}, u32[]{:S(2)}, u32[]{:S(2)}) collective-permute-start(f32[12,6,1,128]{0,3,2,1:T(8,128)S(1)} %get-tuple-element.179), channel_id=1, source_target_pairs={{0,4},{4,8},{8,12},{12,0},{1,5},{5,9},{9,13},{13,1},{2,6},{6,10},{... | collective-permute-start | bytes 110600 | tf_op jit(solution)/shard_map/ppermute | solution.py:17
  15.7 11.3 %collective-permute-start.3 = (f32[12,6,1,128]{0,3,2,1:T(8,128)S(1)}, f32[12,6,1,128]{0,3,2,1:T(8,128)S(1)}, u32[]{:S(2)}, u32[]{:S(2)}) collective-permute-start(f32[12,6,1,128]{0,3,2,1:T(8,128)S(1)} %get-tuple-element.178), channel_id=1, source_target_pairs={{4,0},{8,4},{12,8},{0,12},{5,1},{9,5},{13,9},{1,13},{6,2},{10,6},{... | collective-permute-start | bytes 110600 | tf_op jit(solution)/shard_map/ppermute | solution.py:20
  19.0 36.2 %collective-permute-start.8 = (f32[6,8,2,128]{3,1,2,0:T(8,128)}, f32[6,8,2,128]{3,1,2,0:T(8,128)}, u32[]{:S(2)}, u32[]{:S(2)}) collective-permute-start(f32[6,8,2,128]{3,1,2,0:T(8,128)} %copy.639), channel_id=1, source_target_pairs={{0,4},{4,8},{8,12},{12,0},{1,5},{5,9},{9,13},{13,1},{2,6},{6,10},{... | collective-permute-start | bytes 147464 | tf_op jit(solution)/shard_map/ppermute | solution.py:17
  19.9 36.1 %collective-permute-start.9 = (f32[6,8,2,128]{3,1,2,0:T(8,128)}, f32[6,8,2,128]{3,1,2,0:T(8,128)}, u32[]{:S(2)}, u32[]{:S(2)}) collective-permute-start(f32[6,8,2,128]{3,1,2,0:T(8,128)} %copy.640), channel_id=1, source_target_pairs={{4,0},{8,4},{12,8},{0,12},{5,1},{9,5},{13,9},{1,13},{6,2},{10,6},{... | collective-permute-start | bytes 147464 | tf_op jit(solution)/shard_map/ppermute | solution.py:20
  29.6 11.7 %collective-permute-start.4 = (f32[12,6,10,1]{0,3,2,1:T(1,128)S(1)}, f32[12,6,10,1]{0,3,2,1:T(1,128)S(1)}, u32[]{:S(2)}, u32[]{:S(2)}) collective-permute-start(f32[12,6,10,1]{0,3,2,1:T(1,128)S(1)} %get-tuple-element.176), channel_id=1, source_target_pairs={{0,1},{1,2},{2,3},{3,0},{4,5},{5,6},{6,7},{7,4},{8,9},{9,10},{10,1... | collective-permute-start | bytes 8648 | tf_op jit(solution)/shard_map/ppermute | solution.py:17
  31.4 10.6 %collective-permute-start.5 = (f32[12,6,10,1]{0,3,2,1:T(1,128)S(1)}, f32[12,6,10,1]{0,3,2,1:T(1,128)S(1)}, u32[]{:S(2)}, u32[]{:S(2)}) collective-permute-start(f32[12,6,10,1]{0,3,2,1:T(1,128)S(1)} %get-tuple-element.177), channel_id=1, source_target_pairs={{1,0},{2,1},{3,2},{0,3},{5,4},{6,5},{7,6},{4,7},{9,8},{10,9},{11,1... | collective-permute-start | bytes 8648 | tf_op jit(solution)/shard_map/ppermute | solution.py:20
  53.1 3.8 %collective-permute-start.11 = (f32[4,1,8,128]{3,2,1,0:T(8,128)S(1)}, f32[4,1,8,128]{3,2,1,0:T(8,128)S(1)}, u32[]{:S(2)}, u32[]{:S(2)}) collective-permute-start(f32[4,1,8,128]{3,2,1,0:T(8,128)S(1)} %get-tuple-element.369), channel_id=1, source_target_pairs={{0,16},{16,0},{1,17},{17,1},{2,18},{18,2},{3,19},{19,3},{4,20},{20... | collective-permute-start | bytes 49160 | tf_op jit(solution)/shard_map/ppermute | solution.py:17
  54.8 3.7 %collective-permute-start.12 = (f32[4,1,8,128]{3,2,1,0:T(8,128)S(1)}, f32[4,1,8,128]{3,2,1,0:T(8,128)S(1)}, u32[]{:S(2)}, u32[]{:S(2)}) collective-permute-start(f32[4,1,8,128]{3,2,1,0:T(8,128)S(1)} %get-tuple-element.370), channel_id=1, source_target_pairs={{16,0},{0,16},{17,1},{1,17},{18,2},{2,18},{19,3},{3,19},{20,4},{4,... | collective-permute-start | bytes 49160 | tf_op jit(solution)/shard_map/ppermute | solution.py:20
  58.6 5.8 %collective-permute-start.13 = (f32[4,6,1,128]{3,2,1,0:T(1,128)S(1)}, f32[4,6,1,128]{3,2,1,0:T(1,128)S(1)}, u32[]{:S(2)}, u32[]{:S(2)}) collective-permute-start(f32[4,6,1,128]{3,2,1,0:T(1,128)S(1)} %get-tuple-element.339), channel_id=1, source_target_pairs={{0,4},{4,8},{8,12},{12,0},{1,5},{5,9},{9,13},{13,1},{2,6},{6,10},{... | collective-permute-start | bytes 36872 | tf_op jit(solution)/shard_map/ppermute | solution.py:17
  58.6 5.8 %collective-permute-start.14 = (f32[4,6,1,128]{3,2,1,0:T(1,128)S(1)}, f32[4,6,1,128]{3,2,1,0:T(1,128)S(1)}, u32[]{:S(2)}, u32[]{:S(2)}) collective-permute-start(f32[4,6,1,128]{3,2,1,0:T(1,128)S(1)} %get-tuple-element.340), channel_id=1, source_target_pairs={{4,0},{8,4},{12,8},{0,12},{5,1},{9,5},{13,9},{1,13},{6,2},{10,6},{... | collective-permute-start | bytes 36872 | tf_op jit(solution)/shard_map/ppermute | solution.py:20
  60.5 11.7 %collective-permute-start.10 = (f32[6,8,12,2]{3,1,2,0:T(8,128)S(1)}, f32[6,8,12,2]{3,1,2,0:T(8,128)S(1)}, u32[]{:S(2)}, u32[]{:S(2)}) collective-permute-start(f32[6,8,12,2]{3,1,2,0:T(8,128)S(1)} %get-tuple-element.266), channel_id=1, source_target_pairs={{0,1},{1,2},{2,3},{3,0},{4,5},{5,6},{6,7},{7,4},{8,9},{9,10},{10,1... | collective-permute-start | bytes 13832 | tf_op jit(solution)/shard_map/ppermute | solution.py:17
  60.6 17.1 %collective-permute-start.17 = (f32[6,8,12,2]{3,1,2,0:T(8,128)S(1)}, f32[6,8,12,2]{3,1,2,0:T(8,128)S(1)}, u32[]{:S(2)}, u32[]{:S(2)}) collective-permute-start(f32[6,8,12,2]{3,1,2,0:T(8,128)S(1)} %get-tuple-element.267), channel_id=1, source_target_pairs={{1,0},{2,1},{3,2},{0,3},{5,4},{6,5},{7,6},{4,7},{9,8},{10,9},{11,1... | collective-permute-start | bytes 13832 | tf_op jit(solution)/shard_map/ppermute | solution.py:20
  64.6 18.2 %collective-permute-start.15 = (f32[4,6,10,1]{3,2,1,0:T(8,128)S(1)}, f32[4,6,10,1]{3,2,1,0:T(8,128)S(1)}, u32[]{:S(2)}, u32[]{:S(2)}) collective-permute-start(f32[4,6,10,1]{3,2,1,0:T(8,128)S(1)} %get-tuple-element.310), channel_id=1, source_target_pairs={{0,1},{1,2},{2,3},{3,0},{4,5},{5,6},{6,7},{7,4},{8,9},{9,10},{10,1... | collective-permute-start | bytes 2888 | tf_op jit(solution)/shard_map/ppermute | solution.py:17
  64.7 19.3 %collective-permute-start.16 = (f32[4,6,10,1]{3,2,1,0:T(8,128)S(1)}, f32[4,6,10,1]{3,2,1,0:T(8,128)S(1)}, u32[]{:S(2)}, u32[]{:S(2)}) collective-permute-start(f32[4,6,10,1]{3,2,1,0:T(8,128)S(1)} %get-tuple-element.311), channel_id=1, source_target_pairs={{1,0},{2,1},{3,2},{0,3},{5,4},{6,5},{7,6},{4,7},{9,8},{10,9},{11,1... | collective-permute-start | bytes 2888 | tf_op jit(solution)/shard_map/ppermute | solution.py:20
  87.3 4.2 %collective-permute-start.18 = (f32[6,2,8,128]{3,2,1,0:T(8,128)S(1)}, f32[6,2,8,128]{3,2,1,0:T(8,128)S(1)}, u32[]{:S(2)}, u32[]{:S(2)}) collective-permute-start(f32[6,2,8,128]{3,2,1,0:T(8,128)S(1)} %get-tuple-element.334), channel_id=1, source_target_pairs={{0,16},{16,0},{1,17},{17,1},{2,18},{18,2},{3,19},{19,3},{4,20},{20... | collective-permute-start | bytes 147464 | tf_op jit(solution)/shard_map/ppermute | solution.py:17
  88.3 4.1 %collective-permute-start.19 = (f32[6,2,8,128]{3,2,1,0:T(8,128)S(1)}, f32[6,2,8,128]{3,2,1,0:T(8,128)S(1)}, u32[]{:S(2)}, u32[]{:S(2)}) collective-permute-start(f32[6,2,8,128]{3,2,1,0:T(8,128)S(1)} %get-tuple-element.335), channel_id=1, source_target_pairs={{16,0},{0,16},{17,1},{1,17},{18,2},{2,18},{19,3},{3,19},{20,4},{4,... | collective-permute-start | bytes 147464 | tf_op jit(solution)/shard_map/ppermute | solution.py:20
  92.5 3.6 %collective-permute-start.20 = (f32[6,8,2,128]{3,1,2,0:T(8,128)S(1)}, f32[6,8,2,128]{3,1,2,0:T(8,128)S(1)}, u32[]{:S(2)}, u32[]{:S(2)}) collective-permute-start(f32[6,8,2,128]{3,1,2,0:T(8,128)S(1)} %copy.641), channel_id=1, source_target_pairs={{0,4},{4,8},{8,12},{12,0},{1,5},{5,9},{9,13},{13,1},{2,6},{6,10},{... | collective-permute-start | bytes 147464 | tf_op jit(solution)/shard_map/ppermute | solution.py:17
  96.3 11.8 %collective-permute-start.22 = (f32[6,8,12,2]{3,1,2,0:T(8,128)S(1)}, f32[6,8,12,2]{3,1,2,0:T(8,128)S(1)}, u32[]{:S(2)}, u32[]{:S(2)}) collective-permute-start(f32[6,8,12,2]{3,1,2,0:T(8,128)S(1)} %get-tuple-element.261), channel_id=1, source_target_pairs={{0,1},{1,2},{2,3},{3,0},{4,5},{5,6},{6,7},{7,4},{8,9},{9,10},{10,1... | collective-permute-start | bytes 13832 | tf_op jit(solution)/shard_map/ppermute | solution.py:17
  96.9 16.1 %collective-permute-start.23 = (f32[6,8,12,2]{3,1,2,0:T(8,128)S(1)}, f32[6,8,12,2]{3,1,2,0:T(8,128)S(1)}, u32[]{:S(2)}, u32[]{:S(2)}) collective-permute-start(f32[6,8,12,2]{3,1,2,0:T(8,128)S(1)} %get-tuple-element.262), channel_id=1, source_target_pairs={{1,0},{2,1},{3,2},{0,3},{5,4},{6,5},{7,6},{4,7},{9,8},{10,9},{11,1... | collective-permute-start | bytes 13832 | tf_op jit(solution)/shard_map/ppermute | solution.py:20
  116.0 4.6 %collective-permute-start.25 = (f32[6,2,8,128]{3,2,1,0:T(8,128)S(1)}, f32[6,2,8,128]{3,2,1,0:T(8,128)S(1)}, u32[]{:S(2)}, u32[]{:S(2)}) collective-permute-start(f32[6,2,8,128]{3,2,1,0:T(8,128)S(1)} %get-tuple-element.333), channel_id=1, source_target_pairs={{16,0},{0,16},{17,1},{1,17},{18,2},{2,18},{19,3},{3,19},{20,4},{4,... | collective-permute-start | bytes 147464 | tf_op jit(solution)/shard_map/ppermute | solution.py:20
  117.4 4.1 %collective-permute-start.24 = (f32[6,2,8,128]{3,2,1,0:T(8,128)S(1)}, f32[6,2,8,128]{3,2,1,0:T(8,128)S(1)}, u32[]{:S(2)}, u32[]{:S(2)}) collective-permute-start(f32[6,2,8,128]{3,2,1,0:T(8,128)S(1)} %get-tuple-element.332), channel_id=1, source_target_pairs={{0,16},{16,0},{1,17},{17,1},{2,18},{18,2},{3,19},{19,3},{4,20},{20... | collective-permute-start | bytes 147464 | tf_op jit(solution)/shard_map/ppermute | solution.py:17
  121.6 3.6 %collective-permute-start.26 = (f32[6,8,2,128]{3,1,2,0:T(8,128)S(1)}, f32[6,8,2,128]{3,1,2,0:T(8,128)S(1)}, u32[]{:S(2)}, u32[]{:S(2)}) collective-permute-start(f32[6,8,2,128]{3,1,2,0:T(8,128)S(1)} %copy.643), channel_id=1, source_target_pairs={{0,4},{4,8},{8,12},{12,0},{1,5},{5,9},{9,13},{13,1},{2,6},{6,10},{... | collective-permute-start | bytes 147464 | tf_op jit(solution)/shard_map/ppermute | solution.py:17
  125.5 9.7 %collective-permute-start.28 = (f32[6,8,12,2]{3,1,2,0:T(8,128)S(1)}, f32[6,8,12,2]{3,1,2,0:T(8,128)S(1)}, u32[]{:S(2)}, u32[]{:S(2)}) collective-permute-start(f32[6,8,12,2]{3,1,2,0:T(8,128)S(1)} %get-tuple-element.257), channel_id=1, source_target_pairs={{1,0},{2,1},{3,2},{0,3},{5,4},{6,5},{7,6},{4,7},{9,8},{10,9},{11,1... | collective-permute-start | bytes 13832 | tf_op jit(solution)/shard_map/ppermute | solution.py:20
  127.6 14.8 %collective-permute-start.29 = (f32[6,8,12,2]{3,1,2,0:T(8,128)S(1)}, f32[6,8,12,2]{3,1,2,0:T(8,128)S(1)}, u32[]{:S(2)}, u32[]{:S(2)}) collective-permute-start(f32[6,8,12,2]{3,1,2,0:T(8,128)S(1)} %get-tuple-element.256), channel_id=1, source_target_pairs={{0,1},{1,2},{2,3},{3,0},{4,5},{5,6},{6,7},{7,4},{8,9},{9,10},{10,1... | collective-permute-start | bytes 13832 | tf_op jit(solution)/shard_map/ppermute | solution.py:17
  145.1 4.2 %collective-permute-start.31 = (f32[6,2,8,128]{3,2,1,0:T(8,128)S(1)}, f32[6,2,8,128]{3,2,1,0:T(8,128)S(1)}, u32[]{:S(2)}, u32[]{:S(2)}) collective-permute-start(f32[6,2,8,128]{3,2,1,0:T(8,128)S(1)} %get-tuple-element.331), channel_id=1, source_target_pairs={{16,0},{0,16},{17,1},{1,17},{18,2},{2,18},{19,3},{3,19},{20,4},{4,... | collective-permute-start | bytes 147464 | tf_op jit(solution)/shard_map/ppermute | solution.py:20
  146.1 4.1 %collective-permute-start.30 = (f32[6,2,8,128]{3,2,1,0:T(8,128)S(1)}, f32[6,2,8,128]{3,2,1,0:T(8,128)S(1)}, u32[]{:S(2)}, u32[]{:S(2)}) collective-permute-start(f32[6,2,8,128]{3,2,1,0:T(8,128)S(1)} %get-tuple-element.330), channel_id=1, source_target_pairs={{0,16},{16,0},{1,17},{17,1},{2,18},{18,2},{3,19},{19,3},{4,20},{20... | collective-permute-start | bytes 147464 | tf_op jit(solution)/shard_map/ppermute | solution.py:17
  154.0 9.5 %collective-permute-start.34 = (f32[6,8,12,2]{3,1,2,0:T(8,128)S(1)}, f32[6,8,12,2]{3,1,2,0:T(8,128)S(1)}, u32[]{:S(2)}, u32[]{:S(2)}) collective-permute-start(f32[6,8,12,2]{3,1,2,0:T(8,128)S(1)} %get-tuple-element.252), channel_id=1, source_target_pairs={{1,0},{2,1},{3,2},{0,3},{5,4},{6,5},{7,6},{4,7},{9,8},{10,9},{11,1... | collective-permute-start | bytes 13832 | tf_op jit(solution)/shard_map/ppermute | solution.py:20
  155.7 15.9 %collective-permute-start.35 = (f32[6,8,12,2]{3,1,2,0:T(8,128)S(1)}, f32[6,8,12,2]{3,1,2,0:T(8,128)S(1)}, u32[]{:S(2)}, u32[]{:S(2)}) collective-permute-start(f32[6,8,12,2]{3,1,2,0:T(8,128)S(1)} %get-tuple-element.251), channel_id=1, source_target_pairs={{0,1},{1,2},{2,3},{3,0},{4,5},{5,6},{6,7},{7,4},{8,9},{9,10},{10,1... | collective-permute-start | bytes 13832 | tf_op jit(solution)/shard_map/ppermute | solution.py:17
  174.3 4.7 %collective-permute-start.37 = (f32[6,2,8,128]{3,2,1,0:T(8,128)S(1)}, f32[6,2,8,128]{3,2,1,0:T(8,128)S(1)}, u32[]{:S(2)}, u32[]{:S(2)}) collective-permute-start(f32[6,2,8,128]{3,2,1,0:T(8,128)S(1)} %get-tuple-element.329), channel_id=1, source_target_pairs={{16,0},{0,16},{17,1},{1,17},{18,2},{2,18},{19,3},{3,19},{20,4},{4,... | collective-permute-start | bytes 147464 | tf_op jit(solution)/shard_map/ppermute | solution.py:20
  175.5 4.1 %collective-permute-start.36 = (f32[6,2,8,128]{3,2,1,0:T(8,128)S(1)}, f32[6,2,8,128]{3,2,1,0:T(8,128)S(1)}, u32[]{:S(2)}, u32[]{:S(2)}) collective-permute-start(f32[6,2,8,128]{3,2,1,0:T(8,128)S(1)} %get-tuple-element.328), channel_id=1, source_target_pairs={{0,16},{16,0},{1,17},{17,1},{2,18},{18,2},{3,19},{19,3},{4,20},{20... | collective-permute-start | bytes 147464 | tf_op jit(solution)/shard_map/ppermute | solution.py:17
  183.5 9.6 %collective-permute-start.40 = (f32[6,8,12,2]{3,1,2,0:T(8,128)S(1)}, f32[6,8,12,2]{3,1,2,0:T(8,128)S(1)}, u32[]{:S(2)}, u32[]{:S(2)}) collective-permute-start(f32[6,8,12,2]{3,1,2,0:T(8,128)S(1)} %get-tuple-element.247), channel_id=1, source_target_pairs={{1,0},{2,1},{3,2},{0,3},{5,4},{6,5},{7,6},{4,7},{9,8},{10,9},{11,1... | collective-permute-start | bytes 13832 | tf_op jit(solution)/shard_map/ppermute | solution.py:20
  185.3 14.4 %collective-permute-start.41 = (f32[6,8,12,2]{3,1,2,0:T(8,128)S(1)}, f32[6,8,12,2]{3,1,2,0:T(8,128)S(1)}, u32[]{:S(2)}, u32[]{:S(2)}) collective-permute-start(f32[6,8,12,2]{3,1,2,0:T(8,128)S(1)} %get-tuple-element.246), channel_id=1, source_target_pairs={{0,1},{1,2},{2,3},{3,0},{4,5},{5,6},{6,7},{7,4},{8,9},{9,10},{10,1... | collective-permute-start | bytes 13832 | tf_op jit(solution)/shard_map/ppermute | solution.py:17
  202.4 4.4 %collective-permute-start.43 = (f32[6,2,8,128]{3,2,1,0:T(8,128)S(1)}, f32[6,2,8,128]{3,2,1,0:T(8,128)S(1)}, u32[]{:S(2)}, u32[]{:S(2)}) collective-permute-start(f32[6,2,8,128]{3,2,1,0:T(8,128)S(1)} %get-tuple-element.327), channel_id=1, source_target_pairs={{16,0},{0,16},{17,1},{1,17},{18,2},{2,18},{19,3},{3,19},{20,4},{4,... | collective-permute-start | bytes 147464 | tf_op jit(solution)/shard_map/ppermute | solution.py:20
  203.3 4.1 %collective-permute-start.42 = (f32[6,2,8,128]{3,2,1,0:T(8,128)S(1)}, f32[6,2,8,128]{3,2,1,0:T(8,128)S(1)}, u32[]{:S(2)}, u32[]{:S(2)}) collective-permute-start(f32[6,2,8,128]{3,2,1,0:T(8,128)S(1)} %get-tuple-element.326), channel_id=1, source_target_pairs={{0,16},{16,0},{1,17},{17,1},{2,18},{18,2},{3,19},{19,3},{4,20},{20... | collective-permute-start | bytes 147464 | tf_op jit(solution)/shard_map/ppermute | solution.py:17
  211.3 9.8 %collective-permute-start.46 = (f32[6,8,12,2]{3,1,2,0:T(8,128)S(1)}, f32[6,8,12,2]{3,1,2,0:T(8,128)S(1)}, u32[]{:S(2)}, u32[]{:S(2)}) collective-permute-start(f32[6,8,12,2]{3,1,2,0:T(8,128)S(1)} %get-tuple-element.242), channel_id=1, source_target_pairs={{1,0},{2,1},{3,2},{0,3},{5,4},{6,5},{7,6},{4,7},{9,8},{10,9},{11,1... | collective-permute-start | bytes 13832 | tf_op jit(solution)/shard_map/ppermute | solution.py:20
  213.3 14.9 %collective-permute-start.47 = (f32[6,8,12,2]{3,1,2,0:T(8,128)S(1)}, f32[6,8,12,2]{3,1,2,0:T(8,128)S(1)}, u32[]{:S(2)}, u32[]{:S(2)}) collective-permute-start(f32[6,8,12,2]{3,1,2,0:T(8,128)S(1)} %get-tuple-element.241), channel_id=1, source_target_pairs={{0,1},{1,2},{2,3},{3,0},{4,5},{5,6},{6,7},{7,4},{8,9},{9,10},{10,1... | collective-permute-start | bytes 13832 | tf_op jit(solution)/shard_map/ppermute | solution.py:17
  231.0 4.4 %collective-permute-start.48 = (f32[6,2,8,128]{3,2,1,0:T(8,128)S(1)}, f32[6,2,8,128]{3,2,1,0:T(8,128)S(1)}, u32[]{:S(2)}, u32[]{:S(2)}) collective-permute-start(f32[6,2,8,128]{3,2,1,0:T(8,128)S(1)} %get-tuple-element.324), channel_id=1, source_target_pairs={{0,16},{16,0},{1,17},{17,1},{2,18},{18,2},{3,19},{19,3},{4,20},{20... | collective-permute-start | bytes 147464 | tf_op jit(solution)/shard_map/ppermute | solution.py:17
  232.0 4.1 %collective-permute-start.49 = (f32[6,2,8,128]{3,2,1,0:T(8,128)S(1)}, f32[6,2,8,128]{3,2,1,0:T(8,128)S(1)}, u32[]{:S(2)}, u32[]{:S(2)}) collective-permute-start(f32[6,2,8,128]{3,2,1,0:T(8,128)S(1)} %get-tuple-element.325), channel_id=1, source_target_pairs={{16,0},{0,16},{17,1},{1,17},{18,2},{2,18},{19,3},{3,19},{20,4},{4,... | collective-permute-start | bytes 147464 | tf_op jit(solution)/shard_map/ppermute | solution.py:20
  240.1 11.8 %collective-permute-start.52 = (f32[6,8,12,2]{3,1,2,0:T(8,128)S(1)}, f32[6,8,12,2]{3,1,2,0:T(8,128)S(1)}, u32[]{:S(2)}, u32[]{:S(2)}) collective-permute-start(f32[6,8,12,2]{3,1,2,0:T(8,128)S(1)} %get-tuple-element.236), channel_id=1, source_target_pairs={{0,1},{1,2},{2,3},{3,0},{4,5},{5,6},{6,7},{7,4},{8,9},{9,10},{10,1... | collective-permute-start | bytes 13832 | tf_op jit(solution)/shard_map/ppermute | solution.py:17
  241.5 16.0 %collective-permute-start.53 = (f32[6,8,12,2]{3,1,2,0:T(8,128)S(1)}, f32[6,8,12,2]{3,1,2,0:T(8,128)S(1)}, u32[]{:S(2)}, u32[]{:S(2)}) collective-permute-start(f32[6,8,12,2]{3,1,2,0:T(8,128)S(1)} %get-tuple-element.237), channel_id=1, source_target_pairs={{1,0},{2,1},{3,2},{0,3},{5,4},{6,5},{7,6},{4,7},{9,8},{10,9},{11,1... | collective-permute-start | bytes 13832 | tf_op jit(solution)/shard_map/ppermute | solution.py:20
  260.4 4.2 %collective-permute-start.54 = (f32[6,2,8,128]{3,2,1,0:T(8,128)S(1)}, f32[6,2,8,128]{3,2,1,0:T(8,128)S(1)}, u32[]{:S(2)}, u32[]{:S(2)}) collective-permute-start(f32[6,2,8,128]{3,2,1,0:T(8,128)S(1)} %get-tuple-element.322), channel_id=1, source_target_pairs={{0,16},{16,0},{1,17},{17,1},{2,18},{18,2},{3,19},{19,3},{4,20},{20... | collective-permute-start | bytes 147464 | tf_op jit(solution)/shard_map/ppermute | solution.py:17
  261.3 4.1 %collective-permute-start.55 = (f32[6,2,8,128]{3,2,1,0:T(8,128)S(1)}, f32[6,2,8,128]{3,2,1,0:T(8,128)S(1)}, u32[]{:S(2)}, u32[]{:S(2)}) collective-permute-start(f32[6,2,8,128]{3,2,1,0:T(8,128)S(1)} %get-tuple-element.323), channel_id=1, source_target_pairs={{16,0},{0,16},{17,1},{1,17},{18,2},{2,18},{19,3},{3,19},{20,4},{4,... | collective-permute-start | bytes 147464 | tf_op jit(solution)/shard_map/ppermute | solution.py:20
  270.0 11.7 %collective-permute-start.58 = (f32[6,8,12,2]{3,1,2,0:T(8,128)S(1)}, f32[6,8,12,2]{3,1,2,0:T(8,128)S(1)}, u32[]{:S(2)}, u32[]{:S(2)}) collective-permute-start(f32[6,8,12,2]{3,1,2,0:T(8,128)S(1)} %get-tuple-element.231), channel_id=1, source_target_pairs={{0,1},{1,2},{2,3},{3,0},{4,5},{5,6},{6,7},{7,4},{8,9},{9,10},{10,1... | collective-permute-start | bytes 13832 | tf_op jit(solution)/shard_map/ppermute | solution.py:17
  271.0 15.9 %collective-permute-start.59 = (f32[6,8,12,2]{3,1,2,0:T(8,128)S(1)}, f32[6,8,12,2]{3,1,2,0:T(8,128)S(1)}, u32[]{:S(2)}, u32[]{:S(2)}) collective-permute-start(f32[6,8,12,2]{3,1,2,0:T(8,128)S(1)} %get-tuple-element.232), channel_id=1, source_target_pairs={{1,0},{2,1},{3,2},{0,3},{5,4},{6,5},{7,6},{4,7},{9,8},{10,9},{11,1... | collective-permute-start | bytes 13832 | tf_op jit(solution)/shard_map/ppermute | solution.py:20
  (33 other events, 175.5 us)
where the time goes:
time: 291 us
  waiting for transfers between devices  151 us (52%)
  starting transfers between devices  71.5 us (25%)
  other arithmetic  33.5 us (12%)
  local copies, waits for them, and re-layouts  23.2 us (8%)
  matrix products  8.34 us (3%)
    ppermute x30, waiting for transfers between devices, padded_2(): lax.ppermute(lax.slice_in_dim(block, block.shape[dim] - width, None, axis...  82 us
    ppermute x30, waiting for transfers between devices, padded_2(): lax.ppermute(lax.slice_in_dim(block, 0, width, axis=dim), axis, backward)  69.4 us
    ppermute x30, starting transfers between devices, padded_2(): lax.ppermute(lax.slice_in_dim(block, 0, width, axis=dim), axis, backward)  51.7 us
    ppermute x30, starting transfers between devices, padded_2(): lax.ppermute(lax.slice_in_dim(block, block.shape[dim] - width, None, axis...  19.9 us
    reduce_sum x16, other arithmetic, rotate(): square = jnp.sum(field * field, axis=0)  10.2 us
    unnamed x105, local copies, waits for them, and re-layouts  7.16 us
    concatenate x15, local copies, waits for them, and re-layouts, padded_2(): block = jnp.concatenate([low, block, high], axis=dim)  6.02 us
  transfers between devices with their start and end apart: 60, of which 45 were waited for; matrix products, arithmetic and copies ran while one was open for 12% of the time, Pallas kernels for 0%

commit v1 on v0

v1 whole, which is shorter than its diff:
```python
import functools

import jax
import jax.numpy as jnp
import numpy as np
from jax import lax
from jax.experimental import pallas as pl
from jax.experimental.pallas import tpu as pltpu
from jax.sharding import PartitionSpec as P

half_step = 0.1
lattice_step = 0.25
second_shell = 0.5

f32 = jnp.float32
bf16 = jnp.bfloat16
SUB, LANE = 8, 128
SLAB = 32
XL = 4
ORDER = (0, 2, 1, 3)
TILE = (SUB, LANE)


def iota(dim):
    return lax.broadcasted_iota(jnp.int32, TILE, dim)


def odd_mask(par):
    return ((iota(0) + iota(1) + par) & 1) == 1


def lane_block():
    return ((iota(1) + SLAB // 2) // SLAB) & 3


def lanes(v, shift):
    shift = shift % LANE
    return v if shift == 0 else pltpu.roll(v, shift, 1)


def rows(v, shift):
    return pltpu.roll(v, shift % SUB, 0)


def merge_blocks(tiles):
    block = lane_block()
    out = lanes(tiles[0], 0)
    for b in range(1, 4):
        out = jnp.where(block == b, lanes(tiles[b], SLAB * b), out)
    return out


def vmem_call(body, out_shapes, *args, scratch=(), name=None, cost=None):
    spec = pl.BlockSpec(memory_space=pltpu.VMEM)
    return pl.pallas_call(
        body,
        out_shape=tuple(jax.ShapeDtypeStruct(s, d) for s, d in out_shapes),
        in_specs=[spec] * len(args),
        out_specs=tuple(spec for _ in out_shapes),
        scratch_shapes=list(scratch),
        compiler_params=pltpu.CompilerParams(vmem_limit_bytes=56 << 20),
        name=name,
        cost_estimate=cost,
    )(*args)


def pack_body(disp, mom, bit, out):
    for i in range(14):
        if i < 6:
            tiles = [disp[i, x] for x in ORDER]
        elif i < 12:
            tiles = [mom[i - 6, x] for x in ORDER]
        else:
            tiles = [bit[i - 12, x].astype(f32) for x in ORDER]
        out[i] = merge_blocks(tiles)


def halo_body(disp, mom, bit, low, high, slab, brick, xup, xdn, yup, ydn):
    upper = (iota(1) & (SLAB - 1)) >= SLAB // 2
    e0 = odd_mask(0)
    for i in range(14):
        slab[i] = jnp.where(upper, low[i], high[i])
    for p in range(2):
        for k in range(4):
            i = 6 + 3 * p + k if k < 3 else 12 + p
            tiles = [mom[3 * p + k, x] if k < 3 else bit[p, x].astype(f32) for x in range(XL)]
            for xh in range(2):
                even, odd = tiles[2 * xh], tiles[2 * xh + 1]
                brick[xh, 4 * p + k] = jnp.where(e0, odd, even)
                brick[2 + xh, 4 * p + k] = jnp.where(e0, even, odd)
            h = slab[i]
            brick[4, 4 * p + k] = jnp.where(e0, lanes(h, 64), h)
    for i in range(6):
        src = disp if i < 3 else mom
        k = i % 3
        base = 0 if i < 3 else 6
        xup[2 * i] = src[3 + k, XL - 1]
        xup[2 * i + 1] = slab[base + 3 + k]
        xdn[2 * i] = src[k, 0]
        xdn[2 * i + 1] = slab[base + k]
        yup[i] = jnp.zeros(TILE, f32)
        ydn[i] = jnp.zeros(TILE, f32)
        for x in range(XL):
            yup[i, x : x + 1, :] = src[3 + k, x, SUB - 1 : SUB, :]
            ydn[i, x : x + 1, :] = src[k, x, 0:1, :]
        yup[i, XL : XL + 1, :] = slab[base + 3 + k, SUB - 1 : SUB, :]
        ydn[i, XL : XL + 1, :] = slab[base + k, 0:1, :]


def near_tiles(p, disp, mom, slab, xf, yr, xyr, near):
    q = 1 - p
    lane, sub = iota(1), iota(0)
    block = lane_block()
    edge_x = XL - 1 if p == 0 else 0
    for i in range(6):
        src = disp if i < 3 else mom
        k = i % 3
        c = [src[3 * q + k, x] for x in range(XL)]
        h = slab[(0 if i < 3 else 6) + 3 * q + k]
        fc, fh = xf[2 * i], xf[2 * i + 1]

        def wide(row):
            return jnp.broadcast_to(row, TILE)

        for dy in range(2):
            if dy:
                step = 1 if p == 0 else -1
                put = sub == (0 if p == 0 else SUB - 1)
                c = [jnp.where(put, wide(yr[i, x : x + 1, :]), rows(c[x], step)) for x in range(XL)]
                h = jnp.where(put, wide(yr[i, XL : XL + 1, :]), rows(h, step))
                fc = jnp.where(put, wide(xyr[i, edge_x : edge_x + 1, :]), rows(fc, step))
                fh = jnp.where(put, wide(xyr[i, XL : XL + 1, :]), rows(fh, step))
            for dz in range(2):
                if dz == 0:
                    cs, hs, fcs, fhs = c, h, fc, fh
                else:
                    step = 1 if p == 0 else -1
                    seam = LANE - 1 if p == 0 else 0
                    at_seam = lane == seam
                    at_seams = (lane & (SLAB - 1)) == (SLAB - 1 if p == 0 else 0)
                    cs = [
                        lanes(jnp.where(at_seam, lanes(h, -SLAB * ORDER[x]), c[x]), step)
                        for x in range(XL)
                    ]
                    hs = lanes(jnp.where(at_seams, merge_blocks([c[x] for x in ORDER]), h), step)
                    fcs = lanes(jnp.where(at_seam, lanes(fh, -SLAB * ORDER[edge_x]), fc), step)
                    fhs = lanes(jnp.where(at_seams, lanes(fc, SLAB * ORDER[edge_x]), fh), step)
                at = 2 * dy + dz
                line = [fcs] + cs if p == 0 else cs + [fcs]
                for j in range(XL + 1):
                    near[i, at, j] = line[j]
                near[i, at, XL + 1] = hs
                if p == 0:
                    moved = jnp.where(block == 0, lanes(fhs, SLAB), lanes(hs, 2 * SLAB))
                    moved = jnp.where(block == 1, lanes(hs, -SLAB), moved)
                else:
                    moved = jnp.where(block == 3, lanes(fhs, -SLAB), lanes(hs, 2 * SLAB))
                    moved = jnp.where(block == 2, lanes(hs, SLAB), moved)
                near[i, at, XL + 2] = moved


def feature_rows(p, disp, mom, slab, near, table):
    for slot in range(XL + 1):
        if slot < XL:
            own = [disp[3 * p + k, slot] for k in range(3)]
            own += [mom[3 * p + k, slot] for k in range(3)]
        else:
            own = [slab[3 * p + k] for k in range(3)] + [slab[6 + 3 * p + k] for k in range(3)]
        for o in range(8):
            dx, at = o >> 2, o & 3
            if slot == XL:
                j = XL + 1 + dx
            else:
                j = slot + 1 - dx if p == 0 else slot + dx
            for k in range(3):
                table[slot, pl.ds(4 * o + k, SUB, stride=32), :] = near[k, at, j] - own[k]
            dot = own[3] * near[3, at, j] + own[4] * near[4, at, j] + own[5] * near[5, at, j]
            table[slot, pl.ds(4 * o + 3, SUB, stride=32), :] = dot


def network_body(
    disp, mom, vel, slab, xup, xdn, yup, ydn, xyup, xydn, w_in, b_in, w_mid, w_out,
    disp_out, vel_out, cbrick, near, table, heads,
):
    e0 = odd_mask(0)
    for p in range(2):
        args = (xup, yup, xyup) if p == 0 else (xdn, ydn, xydn)
        near_tiles(p, disp, mom, slab, *args, near)
        feature_rows(p, disp, mom, slab, near, table)

        def one(slot, carry):
            for y in range(0, SUB, 2):
                block = jnp.concatenate(
                    [table[slot, 32 * (y + j) : 32 * (y + j + 1), :].astype(bf16) for j in range(2)],
                    axis=1,
                )
                bias = b_in[...]
                first = jnp.dot(w_in[...], block, preferred_element_type=f32)
                u = first + jnp.concatenate([bias, bias], axis=1)
                first = (u + u * jnp.tanh(u)).astype(bf16)
                u = jnp.dot(w_mid[...], first, preferred_element_type=f32)
                second = (u + u * jnp.tanh(u)).astype(bf16)
                out = jnp.dot(w_out[...], second, preferred_element_type=f32)
                for j in range(2):
                    heads[slot, pl.ds(y + j, SUB, stride=SUB), :] = out[:, LANE * j : LANE * (j + 1)]
            return carry

        lax.fori_loop(0, XL + 1, one, 0)
        coupling = []
        for slot in range(XL + 1):
            coupling.append(1.0 + 0.5 * jnp.tanh(heads[slot, 3 * SUB : 4 * SUB, :]))
            if slot < XL:
                for k in range(3):
                    v = vel[3 * p + k, slot] + lattice_step * heads[slot, k * SUB : (k + 1) * SUB, :]
                    vel_out[3 * p + k, slot] = v
                    disp_out[3 * p + k, slot] = disp[3 * p + k, slot] + lattice_step * v
        for xh in range(2):
            even, odd = coupling[2 * xh], coupling[2 * xh + 1]
            cbrick[xh, p] = jnp.where(e0, odd, even)
            cbrick[2 + xh, p] = jnp.where(e0, even, odd)
        cbrick[4, p] = jnp.where(e0, lanes(coupling[4], 64), coupling[4])


def even_fit(func, terms):
    edge = (np.pi / 2) ** 2 * 1.0001
    node = np.cos((np.arange(400) + 0.5) * np.pi / 400)
    w = 0.5 * edge * (1 + node)
    basis = np.stack([w**n for n in range(terms)], 1)
    return [float(c) for c in np.linalg.lstsq(basis, func(np.sqrt(w)), rcond=None)[0]]


SIN = even_fit(lambda r: np.sin(r) / r, 5)
COS = even_fit(np.cos, 5)


def horner(coeffs, w):
    out = coeffs[-1]
    for c in reversed(coeffs[:-1]):
        out = out * w + c
    return out


def rotated(s, b, h):
    square = b[0] * b[0] + b[1] * b[1] + b[2] * b[2]
    inverse = lax.rsqrt(jnp.maximum(square, 1e-30))
    half = (0.5 * h) * (square * inverse)
    turns = jnp.round(half * (1.0 / np.pi))
    rest = (half - turns * 3.140625) - turns * (np.pi - 3.140625)
    w = rest * rest
    sine = horner(SIN, w) * rest * inverse
    cosine = horner(COS, w)
    along = 2.0 * sine * cosine
    across = 2.0 * sine * sine
    inner = across * (b[0] * s[0] + b[1] * s[1] + b[2] * s[2])
    keep = 1.0 - across * square
    cross = (
        b[1] * s[2] - b[2] * s[1],
        b[2] * s[0] - b[0] * s[2],
        b[0] * s[1] - b[1] * s[0],
    )
    return [keep * s[k] + along * cross[k] + inner * b[k] for k in range(3)]


def turns_body(nx, ny, masks, *refs):
    count = len(masks)
    bricks, cbricks = refs[:count], refs[count : 2 * count]
    out = refs[2 * count]
    mc, mh, hb, cc, ch, chb, tc, th, nc, nh = refs[2 * count + 1 :]
    xh_all, groups = 2 * nx, nx // 2
    ix, iy = lax.axis_index("gx"), lax.axis_index("gy")
    lane, sub = iota(1), iota(0)
    block = lane_block()
    first_half = block < 2

    for n, (mx, my) in enumerate(masks):
        bx, by = ix ^ mx, iy ^ my
        for p in range(2):
            for par in range(2):
                for xh in range(2):
                    for k in range(4):
                        mc[p, par, k, by, 2 * bx + xh] = bricks[n][2 * par + xh, 4 * p + k]
                    cc[p, par, by, 2 * bx + xh] = cbricks[n][2 * par + xh, p]
            for k in range(4):
                hb[by, bx, 4 * p + k] = bricks[n][4, 4 * p + k]
            chb[by, bx, p] = cbricks[n][4, p]

    def joined(even, odd):
        return (
            jnp.where(first_half, even, lanes(odd, 64)),
            jnp.where(first_half, lanes(even, 64), odd),
        )

    for y in range(ny):
        for g in range(groups):
            for p in range(2):
                for k in range(4):
                    zero, one = joined(hb[y, 2 * g, 4 * p + k], hb[y, 2 * g + 1, 4 * p + k])
                    mh[p, 0, k, y, g], mh[p, 1, k, y, g] = zero, one
                zero, one = joined(chb[y, 2 * g, p], chb[y, 2 * g + 1, p])
                ch[p, 0, y, g], ch[p, 1, y, g] = zero, one

    def ring(y):
        up = jnp.where(y == ny - 1, 0, y + 1)
        down = jnp.where(y == 0, ny - 1, y - 1)
        return up, down

    def next_block(tiles, g):
        other = tiles[(g + 1) % groups]
        return lanes(jnp.where(block == 0, other, tiles[g]) if groups > 1 else tiles[g], -SLAB)

    def last_block(tiles, g):
        other = tiles[(g - 1) % groups]
        return lanes(jnp.where(block == 3, other, tiles[g]) if groups > 1 else tiles[g], SLAB)

    def z_next(c, h):
        cs = [
            lanes(jnp.where(lane == 0, lanes(h[x // 4], -SLAB * (x % 4)), c[x]), -1)
            for x in range(xh_all)
        ]
        hs = [
            lanes(jnp.where((lane & (SLAB - 1)) == 0, merge_blocks(c[4 * g : 4 * g + 4]), h[g]), -1)
            for g in range(groups)
        ]
        return cs, hs

    def z_last(c, h):
        cs = [
            lanes(jnp.where(lane == LANE - 1, lanes(h[x // 4], -SLAB * (x % 4)), c[x]), 1)
            for x in range(xh_all)
        ]
        hs = [
            lanes(
                jnp.where((lane & (SLAB - 1)) == SLAB - 1, merge_blocks(c[4 * g : 4 * g + 4]), h[g]), 1
            )
            for g in range(groups)
        ]
        return cs, hs

    def near_total(p):
        q = 1 - p
        e0 = odd_mask(0)

        def pairs(y, carry):
            for k in range(3):
                for ref, to, size in ((mc, tc, xh_all), (mh, th, groups)):
                    zero = [ref[q, 0, k, y, j] for j in range(size)]
                    one = [ref[q, 1, k, y, j] for j in range(size)]
                    even = [jnp.where(e0, one[j], zero[j]) for j in range(size)]
                    odd = [jnp.where(e0, zero[j], one[j]) for j in range(size)]
                    for j in range(size):
                        to[0, k, y, j] = zero[j] + one[j]
                        if p == 0:
                            prev = odd[(j - 1) % size] if ref is mc else last_block(odd, j)
                            to[1, k, y, j] = even[j] + prev
                        else:
                            after = even[(j + 1) % size] if ref is mc else next_block(even, j)
                            to[1, k, y, j] = odd[j] + after
            return carry

        lax.fori_loop(0, ny, pairs, 0)

        def sums(y, carry):
            up, down = ring(y)
            for k in range(3):
                got = []
                for t in range(2):
                    v = []
                    for ref, size in ((tc, xh_all), (th, groups)):
                        row = []
                        for j in range(size):
                            own = ref[t, k, y, j]
                            if p == 0:
                                moved = rows(jnp.where(sub == SUB - 1, ref[t, k, down, j], own), 1)
                            else:
                                moved = rows(jnp.where(sub == 0, ref[t, k, up, j], own), -1)
                            row.append(own + moved)
                        v.append(row)
                    cs, hs = z_last(*v) if p == 0 else z_next(*v)
                    got.append(
                        (
                            [v[0][j] + cs[j] for j in range(xh_all)],
                            [v[1][j] + hs[j] for j in range(groups)],
                        )
                    )
                for kind, to, size in ((0, nc, xh_all), (1, nh, groups)):
                    for j in range(size):
                        whole, split = got[0][kind][j], got[1][kind][j]
                        if p == 0:
                            to[0, k, y, j] = jnp.where(e0, whole, split)
                            to[1, k, y, j] = jnp.where(e0, split, whole)
                        else:
                            to[0, k, y, j] = jnp.where(e0, split, whole)
                            to[1, k, y, j] = jnp.where(e0, whole, split)
            return carry

        lax.fori_loop(0, ny, sums, 0)

    def turn(p, par, bit, h):
        opp = 1 - par
        e = odd_mask(par)

        def body(y, carry):
            up, down = ring(y)
            shell_c, shell_h = [], []
            for k in range(3):
                c = [mc[p, opp, k, y, j] for j in range(xh_all)]
                hh = [mh[p, opp, k, y, g] for g in range(groups)]
                cn, hn = z_next(c, hh)
                cl, hl = z_last(c, hh)
                sc, sh = [], []
                for j in range(xh_all):
                    x = c[j] + jnp.where(e, c[(j + 1) % xh_all], c[(j - 1) % xh_all])
                    yp = rows(jnp.where(sub == 0, mc[p, opp, k, up, j], c[j]), -1)
                    ym = rows(jnp.where(sub == SUB - 1, mc[p, opp, k, down, j], c[j]), 1)
                    sc.append(x + (yp + ym) + (cn[j] + cl[j]))
                for g in range(groups):
                    x = hh[g] + jnp.where(e, next_block(hh, g), last_block(hh, g))
                    yp = rows(jnp.where(sub == 0, mh[p, opp, k, up, g], hh[g]), -1)
                    ym = rows(jnp.where(sub == SUB - 1, mh[p, opp, k, down, g], hh[g]), 1)
                    sh.append(x + (yp + ym) + (hn[g] + hl[g]))
                shell_c.append(sc)
                shell_h.append(sh)
            for state, couple, near, shell, size in (
                (mc, cc, nc, shell_c, xh_all),
                (mh, ch, nh, shell_h, groups),
            ):
                for j in range(size):
                    cpl = couple[p, par, y, j]
                    field = [
                        cpl * near[par, k, y, j] + second_shell * shell[k][j] for k in range(3)
                    ]
                    own = [state[p, par, k, y, j] for k in range(3)]
                    new = rotated(own, field, h)
                    hit = state[p, par, 3, y, j] == bit
                    for k in range(3):
                        state[p, par, k, y, j] = jnp.where(hit, new[k], own[k])
            return carry

        lax.fori_loop(0, ny, body, 0)

    def sweep(p, sector, h):
        turn(p, sector & 1, (sector >> 1).astype(f32), h)

    def climb(i, carry):
        sweep(0, i, half_step)
        return carry

    def middle(i, carry):
        sector = 3 - jnp.abs(3 - i)
        sweep(1, sector, jnp.where(i == 3, 2 * half_step, half_step).astype(f32))
        return carry

    def descend(i, carry):
        sweep(0, 3 - i, half_step)
        return carry

    near_total(0)
    lax.fori_loop(0, 4, climb, 0)
    near_total(1)
    lax.fori_loop(0, 7, middle, 0)
    near_total(0)
    lax.fori_loop(0, 4, descend, 0)

    e0 = odd_mask(0)
    for p in range(2):
        for k in range(3):
            for xh in range(2):
                zero = mc[p, 0, k, iy, 2 * ix + xh]
                one = mc[p, 1, k, iy, 2 * ix + xh]
                out[3 * p + k, 2 * xh] = jnp.where(e0, one, zero)
                out[3 * p + k, 2 * xh + 1] = jnp.where(e0, zero, one)


def on_device(nx, ny, nz, displacement, velocity, moments, sector_bit, weight_in, bias_in, weight_mid, weight_out):
    assert displacement.shape == (6, XL, SUB, LANE)
    assert nx % 2 == 0 and nx & (nx - 1) == 0 and ny & (ny - 1) == 0 and ny % 2 == 0
    plane = ("gx", "gy")

    def pairs(move):
        out = []
        for x in range(nx):
            for y in range(ny):
                tx, ty = move(x, y)
                out.append((x * ny + y, tx % nx * ny + ty % ny))
        return out

    def shift(v, dx, dy):
        return lax.ppermute(v, plane, pairs(lambda x, y: (x + dx, y + dy)))

    def swap(v, mx, my):
        return lax.ppermute(v, plane, pairs(lambda x, y: (x ^ mx, y ^ my)))

    def along_z(v, step):
        return lax.ppermute(v, "gz", [(i, (i + step) % nz) for i in range(nz)])

    w_in = (weight_in.T.astype(f32) * 0.5).astype(bf16)
    w_mid = (weight_mid.T.astype(f32) * 0.5).astype(bf16)
    w_out = jnp.pad(weight_out.T, ((0, SUB - 4), (0, 0)))
    hidden = weight_mid.shape[0]
    b_in = jnp.broadcast_to((0.5 * bias_in)[:, None], (hidden, LANE))

    (packed,) = vmem_call(
        pack_body, [((14, *TILE), f32)], displacement, moments, sector_bit, name="pack"
    )
    low, high = along_z(packed, 1), along_z(packed, -1)
    slab, brick, xup, xdn, yup, ydn = vmem_call(
        halo_body,
        [((14, *TILE), f32), ((5, 8, *TILE), f32)] + [((12, *TILE), f32)] * 2 + [((6, *TILE), f32)] * 2,
        displacement, moments, sector_bit, low, high,
        name="halo",
    )
    xup, xdn = shift(xup, 1, 0), shift(xdn, -1, 0)
    xyup, xydn = shift(yup, 1, 1), shift(ydn, -1, -1)
    yup, ydn = shift(yup, 0, 1), shift(ydn, 0, -1)

    far = [(mx, my) for mx in range(nx) for my in range(0, ny, 2) if mx or my]
    held = {(0, 0): brick}
    for mask in far:
        held[mask] = swap(brick, *mask)
    for mx, my in [(0, 0)] + far:
        held[mx, my + 1] = swap(held[mx, my], 0, 1)

    disp_out, vel_out, cbrick = vmem_call(
        network_body,
        [((6, XL, *TILE), f32), ((6, XL, *TILE), f32), ((5, 2, *TILE), f32)],
        displacement, moments, velocity, slab, xup, xdn, yup, ydn, xyup, xydn, w_in, b_in, w_mid, w_out,
        scratch=[
            pltpu.VMEM((6, 4, XL + 3, *TILE), f32),
            pltpu.VMEM((XL + 1, 32 * SUB, LANE), f32),
            pltpu.VMEM((XL + 1, SUB * SUB, LANE), f32),
        ],
        name="network",
    )
    cheld = {(0, 0): cbrick}
    for mask in far:
        cheld[mask] = swap(cbrick, *mask)
    for mx, my in [(0, 0)] + far:
        cheld[mx, my + 1] = swap(cheld[mx, my], 0, 1)

    masks = sorted(held)
    xh_all, groups = 2 * nx, nx // 2
    (moments_out,) = vmem_call(
        functools.partial(turns_body, nx, ny, masks),
        [((6, XL, *TILE), f32)],
        *[held[m] for m in masks],
        *[cheld[m] for m in masks],
        scratch=[
            pltpu.VMEM((2, 2, 4, ny, xh_all, *TILE), f32),
            pltpu.VMEM((2, 2, 4, ny, groups, *TILE), f32),
            pltpu.VMEM((ny, nx, 8, *TILE), f32),
            pltpu.VMEM((2, 2, ny, xh_all, *TILE), f32),
            pltpu.VMEM((2, 2, ny, groups, *TILE), f32),
            pltpu.VMEM((ny, nx, 2, *TILE), f32),
            pltpu.VMEM((2, 3, ny, xh_all, *TILE), f32),
            pltpu.VMEM((2, 3, ny, groups, *TILE), f32),
            pltpu.VMEM((2, 3, ny, xh_all, *TILE), f32),
            pltpu.VMEM((2, 3, ny, groups, *TILE), f32),
        ],
        name="turns",
    )
    return disp_out, vel_out, moments_out


def solution(mesh):
    placed = P(None, "gx", "gy", "gz")
    sizes = [mesh.shape[axis] for axis in ("gx", "gy", "gz")]
    return jax.shard_map(
        functools.partial(on_device, *sizes),
        mesh=mesh,
        in_specs=(placed,) * 4 + (P(),) * 4,
        out_specs=(placed,) * 3,
        check_vma=False,
    )
```

time: 291 us -> 88.5 us (0.30)
  waiting for transfers between devices: 151 us -> 20.3 us
  starting transfers between devices: 71.5 us -> 19.4 us
  Pallas kernels: 0 us -> 42.5 us
  other arithmetic: 33.5 us -> 1.32 us
  local copies, waits for them, and re-layouts: 23.2 us -> 3.78 us
  matrix products: 8.34 us -> 0 us
    ppermute x60 -> x22, waiting for transfers between devices: 151 us -> 20.3 us  [the longest x14 8.53 us: swap(): return lax.ppermute(v, plane, pairs(lambda x, y: (x ^ mx, y ^ my)))]
    ppermute x60 -> x22, starting transfers between devices: 71.5 us -> 19.4 us  [the longest x14 8.96 us: swap(): return lax.ppermute(v, plane, pairs(lambda x, y: (x ^ mx, y ^ my)))]
    pallas_call x0 -> x4, Pallas kernels: none -> 42.5 us  [vmem_call(): pl.pallas_call(body, out_shape=tuple((jax.ShapeDtypeStruct(s, d) for s, d...]
    reduce_sum x17 -> x0, other arithmetic: 10.7 us -> none  [the longest x16 10.2 us: rotate(): square = jnp.sum(field * field, axis=0)]
    dot_general x16 -> x0, matrix products: 8.34 us -> none  [the longest x8 4.5 us: network(): lax.dot_general(weight_out, second, dims, preferred_element_type=jnp.floa...]
    concatenate x23 -> x0, local copies, waits for them, and re-layouts: 6.97 us -> none  [the longest x15 6.02 us: padded_2(): block = jnp.concatenate([low, block, high], axis=dim)]
    concatenate x31 -> x0, other arithmetic: 6.28 us -> none  [the longest x28 5.62 us: padded_2(): block = jnp.concatenate([low, block, high], axis=dim)]
    cos x16 -> x0, other arithmetic: 5.57 us -> none  [rotate(): jnp.cos(theta) * moment + step * along * cross]
  transfers between devices with their start and end apart: 60 -> 22, of which waited for: 45 -> 9; matrix products, arithmetic and copies ran while one was open for 12% -> 3% of each run, Pallas kernels for 0% -> 23%
where the time goes in v1:
time: 88.5 us; the launch traced here: 88.2 us
  Pallas kernels  42.5 us (48%)
  waiting for transfers between devices  20.3 us (23%)
  starting transfers between devices  19.4 us (22%)
  local copies, waits for them, and re-layouts  3.78 us (4%)
  other arithmetic  1.32 us (1%)
    pallas_call x4, Pallas kernels, vmem_call(): pl.pallas_call(body, out_shape=tuple((jax.ShapeDtypeStruct(s, d) for s, d...  42.5 us
    ppermute x14, starting transfers between devices, swap(): return lax.ppermute(v, plane, pairs(lambda x, y: (x ^ mx, y ^ my)))  8.96 us
    ppermute x14, waiting for transfers between devices, swap(): return lax.ppermute(v, plane, pairs(lambda x, y: (x ^ mx, y ^ my)))  8.53 us
    ppermute x6, waiting for transfers between devices, shift(): return lax.ppermute(v, plane, pairs(lambda x, y: (x + dx, y + dy)))  6.52 us
    ppermute x6, starting transfers between devices, shift(): return lax.ppermute(v, plane, pairs(lambda x, y: (x + dx, y + dy)))  5.37 us
    ppermute x2, waiting for transfers between devices, along_z(): return lax.ppermute(v, 'gz', [(i, (i + step) % nz) for i in range(nz)])  5.25 us
    ppermute x2, starting transfers between devices, along_z(): return lax.ppermute(v, 'gz', [(i, (i + step) % nz) for i in range(nz)])  5.08 us
    unnamed x55, local copies, waits for them, and re-layouts  2.34 us
  transfers between devices with their start and end apart: 22, of which 9 were waited for; matrix products, arithmetic and copies ran while one was open for 3% of the time, Pallas kernels for 23%

profile of v1, /device:TPU:0, one launch (start us, length us, event | category | flops | bytes accessed | tf_op | source)
XLA Modules:
  0.0 88.2 jit_solution(11918969206860274844)
XLA Ops:
  0.6 1.7 %pack.1 = f32[14,8,128]{2,1,0:T(8,128)} custom-call(f32[6,4,8,128]{3,2,1,0:T(8,128)} %disp.5, f32[6,4,8,128]{3,2,1,0:T(8,128)} %mom.5, s32[2,4,8,128]{3,2,1,0:T(8,128)} %bit.3), custom_call_target="tpu_custom_call" | custom-call | tf_op jit(solution)/shard_map/pack/pallas_call | solution.py:55
  2.4 5.1 %collective-permute-start.1 = (f32[14,8,128]{2,1,0:T(8,128)}, f32[14,8,128]{2,1,0:T(8,128)S(1)}, u32[]{:S(2)}, u32[]{:S(2)}) collective-permute-start(f32[14,8,128]{2,1,0:T(8,128)} %pack.1), channel_id=1, source_target_pairs={{0,3},{1,0},{2,1},{3,2},{4,7},{5,4},{6,5},{7,6},{8,11},{9,8},{10,9... | collective-permute-start | bytes 172040 | tf_op jit(solution)/shard_map/ppermute | solution.py:494
  7.4 0.0 collective-permute-start
  7.4 0.1 copy.14
  7.5 0.0 copy-start.24
  7.6 0.7 fusion.w_mid
  8.2 0.0 copy-done.24
  8.3 0.1 copy.13
  8.4 1.2 %collective-permute-done.1.high = f32[14,8,128]{2,1,0:T(8,128)S(1)} collective-permute-done((f32[14,8,128]{2,1,0:T(8,128)}, f32[14,8,128]{2,1,0:T(8,128)S(1)}, u32[]{:S(2)}, u32[]{:S(2)}) %collective-permute-start.1) | collective-permute-done | bytes 57376 | tf_op jit(solution)/shard_map/ppermute | solution.py:494
  9.6 4.0 %collective-permute-done.low = f32[14,8,128]{2,1,0:T(8,128)S(1)} collective-permute-done((f32[14,8,128]{2,1,0:T(8,128)}, f32[14,8,128]{2,1,0:T(8,128)S(1)}, u32[]{:S(2)}, u32[]{:S(2)}) %collective-permute-start) | collective-permute-done | bytes 57376 | tf_op jit(solution)/shard_map/ppermute | solution.py:494
  13.6 0.6 copy-done.10
  14.2 1.7 %halo.1 = (f32[14,8,128]{2,1,0:T(8,128)}, f32[5,8,8,128]{3,2,1,0:T(8,128)}, f32[12,8,128]{2,1,0:T(8,128)}, f32[12,8,128]{2,1,0:T(8,128)}, f32[6,8,128]{2,1,0:T(8,128)}, /*index=5*/f32[6,8,128]{2,1,0:T(8,128)}) custom-call(f32[6,4,8,128]{3,2,1,0:T(8,128)} %disp.5, f32[6,4,8,128]{3,2,1,0:T(8,128)} %mom.5, s32[2,4,8,128]{3,2,1,0:T(8,128)} %bit.3, ...), custom_call_target="tpu_custom_call" | custom-call | tf_op jit(solution)/shard_map/halo/pallas_call | solution.py:55
  16.0 0.0 collective-permute-start.6
  16.0 2.5 %collective-permute-start.4 = (f32[6,8,128]{2,1,0:T(8,128)}, f32[6,8,128]{2,1,0:T(8,128)S(1)}, u32[]{:S(2)}, u32[]{:S(2)}) collective-permute-start(f32[6,8,128]{2,1,0:T(8,128)} %get-tuple-element.15), channel_id=1, source_target_pairs={{0,4},{4,8},{8,12},{12,0},{16,20},{20,24},{24,28},{28,16},{1,5},{5... | collective-permute-start | bytes 73736 | tf_op jit(solution)/shard_map/ppermute | solution.py:488
  18.6 0.2 collective-permute-start.7
  18.8 0.6 collective-permute-start.5
  19.3 0.6 fusion.1.w_in
  20.0 2.4 %collective-permute-start.13 = (f32[5,8,8,128]{3,2,1,0:T(8,128)S(1)}, f32[5,8,8,128]{3,2,1,0:T(8,128)S(1)}, u32[]{:S(2)}, u32[]{:S(2)}) collective-permute-start(f32[5,8,8,128]{3,2,1,0:T(8,128)S(1)} %copy-done), channel_id=1, source_target_pairs={{0,24},{4,28},{8,16},{12,20},{16,8},{20,12},{24,0},{28,4},{1,25},{... | collective-permute-start | bytes 491528 | tf_op jit(solution)/shard_map/ppermute | solution.py:491
  22.4 0.5 collective-permute-start.11
  22.9 0.5 collective-permute-start.9
  23.5 1.5 %collective-permute-start.2 = (f32[12,8,128]{2,1,0:T(8,128)}, f32[12,8,128]{2,1,0:T(8,128)S(1)}, u32[]{:S(2)}, u32[]{:S(2)}) collective-permute-start(f32[12,8,128]{2,1,0:T(8,128)} %get-tuple-element.13), channel_id=1, source_target_pairs={{0,16},{4,20},{8,24},{12,28},{16,0},{20,4},{24,8},{28,12},{1,17},{... | collective-permute-start | bytes 147464 | tf_op jit(solution)/shard_map/ppermute | solution.py:488
  25.0 0.5 collective-permute-start.3
  25.5 0.2 copy-done.25
  25.7 0.6 pad.4.w_out
  26.3 5.5 %collective-permute-done.2.xup = f32[12,8,128]{2,1,0:T(8,128)S(1)} collective-permute-done((f32[12,8,128]{2,1,0:T(8,128)}, f32[12,8,128]{2,1,0:T(8,128)S(1)}, u32[]{:S(2)}, u32[]{:S(2)}) %collective-permute-start.2) | collective-permute-done | bytes 49184 | tf_op jit(solution)/shard_map/ppermute | solution.py:488
  31.9 1.0 %collective-permute-done.3.xdn = f32[12,8,128]{2,1,0:T(8,128)S(1)} collective-permute-done((f32[12,8,128]{2,1,0:T(8,128)}, f32[12,8,128]{2,1,0:T(8,128)S(1)}, u32[]{:S(2)}, u32[]{:S(2)}) %collective-permute-start.3) | collective-permute-done | bytes 49184 | tf_op jit(solution)/shard_map/ppermute | solution.py:488
  32.8 0.7 broadcast_in_dim.2.b_in
  33.6 20.4 %network.1 = (f32[6,4,8,128]{3,2,1,0:T(8,128)}, f32[6,4,8,128]{3,2,1,0:T(8,128)}, f32[5,2,8,128]{3,2,1,0:T(8,128)}) custom-call(f32[6,4,8,128]{3,2,1,0:T(8,128)} %disp.5, f32[6,4,8,128]{3,2,1,0:T(8,128)} %mom.5, f32[6,4,8,128]{3,2,1,0:T(8,128)} %vel.1, f32[14,8,128]{2,1,0:T(8,128)} %get-tuple-element.12.slab, f32[12,8,128]{2,1,0:T(8,128)} %copy-done.11, ...), custom_call_target="tpu_custom_call" | custom-call | tf_op jit(solution)/shard_map/network/pallas_call | solution.py:55
  54.0 1.5 %collective-permute-start.20 = (f32[5,2,8,128]{3,2,1,0:T(8,128)}, f32[5,2,8,128]{3,2,1,0:T(8,128)S(1)}, u32[]{:S(2)}, u32[]{:S(2)}) collective-permute-start(f32[5,2,8,128]{3,2,1,0:T(8,128)} %get-tuple-element.20.refs_8_), channel_id=1, source_target_pairs={{0,24},{4,28},{8,16},{12,20},{16,8},{20,12},{24,0},{28,4},{1,25},{... | collective-permute-start | bytes 122888 | tf_op jit(solution)/shard_map/ppermute | solution.py:491
  55.4 1.2 %collective-permute-start.18 = (f32[5,2,8,128]{3,2,1,0:T(8,128)}, f32[5,2,8,128]{3,2,1,0:T(8,128)S(1)}, u32[]{:S(2)}, u32[]{:S(2)}) collective-permute-start(f32[5,2,8,128]{3,2,1,0:T(8,128)} %get-tuple-element.20.refs_8_), channel_id=1, source_target_pairs={{0,16},{4,20},{8,24},{12,28},{16,0},{20,4},{24,8},{28,12},{1,17},{... | collective-permute-start | bytes 122888 | tf_op jit(solution)/shard_map/ppermute | solution.py:491
  56.7 2.4 %collective-permute-done.20.refs_14_ = f32[5,2,8,128]{3,2,1,0:T(8,128)S(1)} collective-permute-done((f32[5,2,8,128]{3,2,1,0:T(8,128)}, f32[5,2,8,128]{3,2,1,0:T(8,128)S(1)}, u32[]{:S(2)}, u32[]{:S(2)}) %collective-permute-start.20) | collective-permute-done | bytes 40992 | tf_op jit(solution)/shard_map/ppermute | solution.py:491
  59.1 1.2 %collective-permute-start.16 = (f32[5,2,8,128]{3,2,1,0:T(8,128)}, f32[5,2,8,128]{3,2,1,0:T(8,128)S(1)}, u32[]{:S(2)}, u32[]{:S(2)}) collective-permute-start(f32[5,2,8,128]{3,2,1,0:T(8,128)} %get-tuple-element.20.refs_8_), channel_id=1, source_target_pairs={{0,8},{4,12},{8,0},{12,4},{16,24},{20,28},{24,16},{28,20},{1,9},{5... | collective-permute-start | bytes 122888 | tf_op jit(solution)/shard_map/ppermute | solution.py:491
  60.3 3.0 %collective-permute-done.16.refs_10_ = f32[5,2,8,128]{3,2,1,0:T(8,128)S(1)} collective-permute-done((f32[5,2,8,128]{3,2,1,0:T(8,128)}, f32[5,2,8,128]{3,2,1,0:T(8,128)S(1)}, u32[]{:S(2)}, u32[]{:S(2)}) %collective-permute-start.16) | collective-permute-done | bytes 40992 | tf_op jit(solution)/shard_map/ppermute | solution.py:491
  63.3 0.5 collective-permute-start.14
  63.8 0.1 collective-permute-start.12
  63.9 0.4 collective-permute-start.10
  64.3 0.1 collective-permute-start.21
  64.4 1.1 %collective-permute-done.21.refs_15_ = f32[5,2,8,128]{3,2,1,0:T(8,128)S(1)} collective-permute-done((f32[5,2,8,128]{3,2,1,0:T(8,128)S(1)}, f32[5,2,8,128]{3,2,1,0:T(8,128)S(1)}, u32[]{:S(2)}, u32[]{:S(2)}) %collective-permute-start.21) | collective-permute-done | bytes 40992 | tf_op jit(solution)/shard_map/ppermute | solution.py:491
  65.6 0.2 collective-permute-start.19
  65.8 1.0 %collective-permute-done.19.refs_13_ = f32[5,2,8,128]{3,2,1,0:T(8,128)S(1)} collective-permute-done((f32[5,2,8,128]{3,2,1,0:T(8,128)S(1)}, f32[5,2,8,128]{3,2,1,0:T(8,128)S(1)}, u32[]{:S(2)}, u32[]{:S(2)}) %collective-permute-start.19) | collective-permute-done | bytes 40992 | tf_op jit(solution)/shard_map/ppermute | solution.py:491
  66.8 0.2 collective-permute-start.17
  67.0 1.0 %collective-permute-done.17.refs_11_ = f32[5,2,8,128]{3,2,1,0:T(8,128)S(1)} collective-permute-done((f32[5,2,8,128]{3,2,1,0:T(8,128)S(1)}, f32[5,2,8,128]{3,2,1,0:T(8,128)S(1)}, u32[]{:S(2)}, u32[]{:S(2)}) %collective-permute-start.17) | collective-permute-done | bytes 40992 | tf_op jit(solution)/shard_map/ppermute | solution.py:491
  68.1 0.5 copy-done.19
  68.6 0.1 copy-done.4
  68.7 0.0 copy-done.5
  68.7 0.1 copy-done.6
  68.8 0.7 copy-done.7
  69.5 18.7 %turns.1 = f32[6,4,8,128]{3,2,1,0:T(8,128)} custom-call(f32[5,8,8,128]{3,2,1,0:T(8,128)} %get-tuple-element.19.refs_0_, f32[5,8,8,128]{3,2,1,0:T(8,128)} %copy-done.4, f32[5,8,8,128]{3,2,1,0:T(8,128)} %copy-done.3, f32[5,8,8,128]{3,2,1,0:T(8,128)} %copy-done.7, f32[5,8,8,128]{3,2,1,0:T(8,128)} %copy-done.2, f32[5,8,8,128]{3,2,1,0:T(8,128)} %copy-done.6, ...), custom_call_target="tpu_custom_call" | custom-call | tf_op jit(solution)/shard_map/turns/pallas_call | solution.py:55
  (61 shorter events, 0.1 us)
Async XLA Ops:
  0.6 6.8 %copy-start.8 = (bf16[256,256]{1,0:T(8,128)(2,1)S(1)}, bf16[256,256]{1,0:T(8,128)(2,1)}, u32[]{:S(2)}) copy-start(bf16[256,256]{1,0:T(8,128)(2,1)} %param.14) | copy-start | bytes 393220
  2.4 7.2 %collective-permute-start.1 = (f32[14,8,128]{2,1,0:T(8,128)}, f32[14,8,128]{2,1,0:T(8,128)S(1)}, u32[]{:S(2)}, u32[]{:S(2)}) collective-permute-start(f32[14,8,128]{2,1,0:T(8,128)} %pack.1), channel_id=1, source_target_pairs={{0,3},{1,0},{2,1},{3,2},{4,7},{5,4},{6,5},{7,6},{8,11},{9,8},{10,9... | collective-permute-start | bytes 172040 | tf_op jit(solution)/shard_map/ppermute | solution.py:494
  7.4 6.2 %collective-permute-start = (f32[14,8,128]{2,1,0:T(8,128)}, f32[14,8,128]{2,1,0:T(8,128)S(1)}, u32[]{:S(2)}, u32[]{:S(2)}) collective-permute-start(f32[14,8,128]{2,1,0:T(8,128)} %pack.1), channel_id=1, source_target_pairs={{0,1},{1,2},{2,3},{3,0},{4,5},{5,6},{6,7},{7,4},{8,9},{9,10},{10,1... | collective-permute-start | bytes 172040 | tf_op jit(solution)/shard_map/ppermute | solution.py:494
  7.5 0.7 copy-start.24
  9.6 4.0 %copy-start.9 = (f32[14,8,128]{2,1,0:T(8,128)}, f32[14,8,128]{2,1,0:T(8,128)S(1)}, u32[]{:S(2)}) copy-start(f32[14,8,128]{2,1,0:T(8,128)S(1)} %collective-permute-done.1.high) | copy-start | bytes 172036
  13.6 0.6 copy-start.10
  16.0 4.0 %copy-start = (f32[5,8,8,128]{3,2,1,0:T(8,128)S(1)}, f32[5,8,8,128]{3,2,1,0:T(8,128)}, u32[]{:S(2)}) copy-start(f32[5,8,8,128]{3,2,1,0:T(8,128)} %get-tuple-element.19.refs_0_) | copy-start | bytes 491524
  16.0 6.4 %collective-permute-start.6 = (f32[6,8,128]{2,1,0:T(8,128)}, f32[6,8,128]{2,1,0:T(8,128)S(1)}, u32[]{:S(2)}, u32[]{:S(2)}) collective-permute-start(f32[6,8,128]{2,1,0:T(8,128)} %get-tuple-element.15), channel_id=1, source_target_pairs={{0,20},{4,24},{8,28},{12,16},{16,4},{20,8},{24,12},{28,0},{1,21},{... | collective-permute-start | bytes 73736 | tf_op jit(solution)/shard_map/ppermute | solution.py:488
  16.0 6.9 %collective-permute-start.4 = (f32[6,8,128]{2,1,0:T(8,128)}, f32[6,8,128]{2,1,0:T(8,128)S(1)}, u32[]{:S(2)}, u32[]{:S(2)}) collective-permute-start(f32[6,8,128]{2,1,0:T(8,128)} %get-tuple-element.15), channel_id=1, source_target_pairs={{0,4},{4,8},{8,12},{12,0},{16,20},{20,24},{24,28},{28,16},{1,5},{5... | collective-permute-start | bytes 73736 | tf_op jit(solution)/shard_map/ppermute | solution.py:488
  18.6 4.9 %collective-permute-start.7 = (f32[6,8,128]{2,1,0:T(8,128)}, f32[6,8,128]{2,1,0:T(8,128)S(1)}, u32[]{:S(2)}, u32[]{:S(2)}) collective-permute-start(f32[6,8,128]{2,1,0:T(8,128)} %get-tuple-element.16), channel_id=1, source_target_pairs={{0,28},{4,16},{8,20},{12,24},{16,12},{20,0},{24,4},{28,8},{1,29},{... | collective-permute-start | bytes 73736 | tf_op jit(solution)/shard_map/ppermute | solution.py:488
  18.8 6.2 %collective-permute-start.5 = (f32[6,8,128]{2,1,0:T(8,128)}, f32[6,8,128]{2,1,0:T(8,128)S(1)}, u32[]{:S(2)}, u32[]{:S(2)}) collective-permute-start(f32[6,8,128]{2,1,0:T(8,128)} %get-tuple-element.16), channel_id=1, source_target_pairs={{0,12},{4,0},{8,4},{12,8},{16,28},{20,16},{24,20},{28,24},{1,13},{... | collective-permute-start | bytes 73736 | tf_op jit(solution)/shard_map/ppermute | solution.py:488
  20.0 43.3 %collective-permute-start.13 = (f32[5,8,8,128]{3,2,1,0:T(8,128)S(1)}, f32[5,8,8,128]{3,2,1,0:T(8,128)S(1)}, u32[]{:S(2)}, u32[]{:S(2)}) collective-permute-start(f32[5,8,8,128]{3,2,1,0:T(8,128)S(1)} %copy-done), channel_id=1, source_target_pairs={{0,24},{4,28},{8,16},{12,20},{16,8},{20,12},{24,0},{28,4},{1,25},{... | collective-permute-start | bytes 491528 | tf_op jit(solution)/shard_map/ppermute | solution.py:491
  22.4 11.1 %copy-start.20 = (f32[6,8,128]{2,1,0:T(8,128)}, f32[6,8,128]{2,1,0:T(8,128)S(1)}, u32[]{:S(2)}) copy-start(f32[6,8,128]{2,1,0:T(8,128)S(1)} %collective-permute-done.6.xyup) | copy-start | bytes 73732
  22.4 41.4 %collective-permute-start.11 = (f32[5,8,8,128]{3,2,1,0:T(8,128)S(1)}, f32[5,8,8,128]{3,2,1,0:T(8,128)S(1)}, u32[]{:S(2)}, u32[]{:S(2)}) collective-permute-start(f32[5,8,8,128]{3,2,1,0:T(8,128)S(1)} %copy-done), channel_id=1, source_target_pairs={{0,16},{4,20},{8,24},{12,28},{16,0},{20,4},{24,8},{28,12},{1,17},{... | collective-permute-start | bytes 491528 | tf_op jit(solution)/shard_map/ppermute | solution.py:491
  22.9 10.6 %copy-start.21 = (f32[6,8,128]{2,1,0:T(8,128)}, f32[6,8,128]{2,1,0:T(8,128)S(1)}, u32[]{:S(2)}) copy-start(f32[6,8,128]{2,1,0:T(8,128)S(1)} %collective-permute-done.4.yup) | copy-start | bytes 73732
  22.9 41.0 %collective-permute-start.9 = (f32[5,8,8,128]{3,2,1,0:T(8,128)S(1)}, f32[5,8,8,128]{3,2,1,0:T(8,128)S(1)}, u32[]{:S(2)}, u32[]{:S(2)}) collective-permute-start(f32[5,8,8,128]{3,2,1,0:T(8,128)S(1)} %copy-done), channel_id=1, source_target_pairs={{0,8},{4,12},{8,0},{12,4},{16,24},{20,28},{24,16},{28,20},{1,9},{5... | collective-permute-start | bytes 491528 | tf_op jit(solution)/shard_map/ppermute | solution.py:491
  23.5 10.1 %copy-start.22 = (f32[6,8,128]{2,1,0:T(8,128)}, f32[6,8,128]{2,1,0:T(8,128)S(1)}, u32[]{:S(2)}) copy-start(f32[6,8,128]{2,1,0:T(8,128)S(1)} %collective-permute-done.7.xydn) | copy-start | bytes 73732
  23.5 2.0 %copy-start.26 = (f32[256]{0:T(256)S(1)}, f32[256]{0:T(256)}, u32[]{:S(2)}) copy-start(f32[256]{0:T(256)} %param.13) | copy-start | bytes 3076
  23.5 8.4 %collective-permute-start.2 = (f32[12,8,128]{2,1,0:T(8,128)}, f32[12,8,128]{2,1,0:T(8,128)S(1)}, u32[]{:S(2)}, u32[]{:S(2)}) collective-permute-start(f32[12,8,128]{2,1,0:T(8,128)} %get-tuple-element.13), channel_id=1, source_target_pairs={{0,16},{4,20},{8,24},{12,28},{16,0},{20,4},{24,8},{28,12},{1,17},{... | collective-permute-start | bytes 147464 | tf_op jit(solution)/shard_map/ppermute | solution.py:488
  25.0 8.6 %copy-start.23 = (f32[6,8,128]{2,1,0:T(8,128)}, f32[6,8,128]{2,1,0:T(8,128)S(1)}, u32[]{:S(2)}) copy-start(f32[6,8,128]{2,1,0:T(8,128)S(1)} %collective-permute-done.5.ydn) | copy-start | bytes 73732
  25.0 0.7 copy-start.25
  25.0 7.8 %collective-permute-start.3 = (f32[12,8,128]{2,1,0:T(8,128)}, f32[12,8,128]{2,1,0:T(8,128)S(1)}, u32[]{:S(2)}, u32[]{:S(2)}) collective-permute-start(f32[12,8,128]{2,1,0:T(8,128)} %get-tuple-element.14), channel_id=1, source_target_pairs={{0,16},{4,20},{8,24},{12,28},{16,0},{20,4},{24,8},{28,12},{1,17},{... | collective-permute-start | bytes 147464 | tf_op jit(solution)/shard_map/ppermute | solution.py:488
  31.9 1.7 %copy-start.11 = (f32[12,8,128]{2,1,0:T(8,128)}, f32[12,8,128]{2,1,0:T(8,128)S(1)}, u32[]{:S(2)}) copy-start(f32[12,8,128]{2,1,0:T(8,128)S(1)} %collective-permute-done.2.xup) | copy-start | bytes 147460
  32.8 0.8 copy-start.12
  54.0 5.1 %collective-permute-start.20 = (f32[5,2,8,128]{3,2,1,0:T(8,128)}, f32[5,2,8,128]{3,2,1,0:T(8,128)S(1)}, u32[]{:S(2)}, u32[]{:S(2)}) collective-permute-start(f32[5,2,8,128]{3,2,1,0:T(8,128)} %get-tuple-element.20.refs_8_), channel_id=1, source_target_pairs={{0,24},{4,28},{8,16},{12,20},{16,8},{20,12},{24,0},{28,4},{1,25},{... | collective-permute-start | bytes 122888 | tf_op jit(solution)/shard_map/ppermute | solution.py:491
  55.4 4.9 %collective-permute-start.18 = (f32[5,2,8,128]{3,2,1,0:T(8,128)}, f32[5,2,8,128]{3,2,1,0:T(8,128)S(1)}, u32[]{:S(2)}, u32[]{:S(2)}) collective-permute-start(f32[5,2,8,128]{3,2,1,0:T(8,128)} %get-tuple-element.20.refs_8_), channel_id=1, source_target_pairs={{0,16},{4,20},{8,24},{12,28},{16,0},{20,4},{24,8},{28,12},{1,17},{... | collective-permute-start | bytes 122888 | tf_op jit(solution)/shard_map/ppermute | solution.py:491
  59.1 9.0 %copy-start.13 = (f32[5,2,8,128]{3,2,1,0:T(8,128)}, f32[5,2,8,128]{3,2,1,0:T(8,128)S(1)}, u32[]{:S(2)}) copy-start(f32[5,2,8,128]{3,2,1,0:T(8,128)S(1)} %collective-permute-done.20.refs_14_) | copy-start | bytes 122884
  59.1 4.2 %collective-permute-start.16 = (f32[5,2,8,128]{3,2,1,0:T(8,128)}, f32[5,2,8,128]{3,2,1,0:T(8,128)S(1)}, u32[]{:S(2)}, u32[]{:S(2)}) collective-permute-start(f32[5,2,8,128]{3,2,1,0:T(8,128)} %get-tuple-element.20.refs_8_), channel_id=1, source_target_pairs={{0,8},{4,12},{8,0},{12,4},{16,24},{20,28},{24,16},{28,20},{1,9},{5... | collective-permute-start | bytes 122888 | tf_op jit(solution)/shard_map/ppermute | solution.py:491
  60.3 7.8 %copy-start.14 = (f32[5,2,8,128]{3,2,1,0:T(8,128)}, f32[5,2,8,128]{3,2,1,0:T(8,128)S(1)}, u32[]{:S(2)}) copy-start(f32[5,2,8,128]{3,2,1,0:T(8,128)S(1)} %collective-permute-done.18.refs_12_) | copy-start | bytes 122884
  60.3 4.0 %collective-permute-start.15 = (f32[5,2,8,128]{3,2,1,0:T(8,128)}, f32[5,2,8,128]{3,2,1,0:T(8,128)S(1)}, u32[]{:S(2)}, u32[]{:S(2)}) collective-permute-start(f32[5,2,8,128]{3,2,1,0:T(8,128)} %get-tuple-element.20.refs_8_), channel_id=1, source_target_pairs={{0,4},{4,0},{8,12},{12,8},{16,20},{20,16},{24,28},{28,24},{1,5},{5... | collective-permute-start | bytes 122888 | tf_op jit(solution)/shard_map/ppermute | solution.py:491
  63.3 4.8 %copy-start.15 = (f32[5,2,8,128]{3,2,1,0:T(8,128)}, f32[5,2,8,128]{3,2,1,0:T(8,128)S(1)}, u32[]{:S(2)}) copy-start(f32[5,2,8,128]{3,2,1,0:T(8,128)S(1)} %collective-permute-done.16.refs_10_) | copy-start | bytes 122884
  63.3 4.7 %collective-permute-start.8 = (f32[5,8,8,128]{3,2,1,0:T(8,128)S(1)}, f32[5,8,8,128]{3,2,1,0:T(8,128)S(1)}, u32[]{:S(2)}, u32[]{:S(2)}) collective-permute-start(f32[5,8,8,128]{3,2,1,0:T(8,128)S(1)} %copy-done), channel_id=1, source_target_pairs={{0,4},{4,0},{8,12},{12,8},{16,20},{20,16},{24,28},{28,24},{1,5},{5... | collective-permute-start | bytes 491528 | tf_op jit(solution)/shard_map/ppermute | solution.py:491
  63.3 4.8 %copy-start.1 = (f32[5,8,8,128]{3,2,1,0:T(8,128)}, f32[5,8,8,128]{3,2,1,0:T(8,128)S(1)}, u32[]{:S(2)}) copy-start(f32[5,8,8,128]{3,2,1,0:T(8,128)S(1)} %collective-permute-done.13.refs_6_) | copy-start | bytes 491524
  63.3 4.7 %collective-permute-start.14 = (f32[5,8,8,128]{3,2,1,0:T(8,128)S(1)}, f32[5,8,8,128]{3,2,1,0:T(8,128)S(1)}, u32[]{:S(2)}, u32[]{:S(2)}) collective-permute-start(f32[5,8,8,128]{3,2,1,0:T(8,128)S(1)} %collective-permute-done.13.refs_6_), channel_id=1, source_target_pairs={{0,4},{4,0},{8,12},{12,8},{16,20},{20,16},{24,28},{28,24},{1,5},{5... | collective-permute-start | bytes 491528 | tf_op jit(solution)/shard_map/ppermute | solution.py:491
  63.8 4.3 %copy-start.2 = (f32[5,8,8,128]{3,2,1,0:T(8,128)}, f32[5,8,8,128]{3,2,1,0:T(8,128)S(1)}, u32[]{:S(2)}) copy-start(f32[5,8,8,128]{3,2,1,0:T(8,128)S(1)} %collective-permute-done.11.refs_4_) | copy-start | bytes 491524
  63.8 4.2 %collective-permute-start.12 = (f32[5,8,8,128]{3,2,1,0:T(8,128)S(1)}, f32[5,8,8,128]{3,2,1,0:T(8,128)S(1)}, u32[]{:S(2)}, u32[]{:S(2)}) collective-permute-start(f32[5,8,8,128]{3,2,1,0:T(8,128)S(1)} %collective-permute-done.11.refs_4_), channel_id=1, source_target_pairs={{0,4},{4,0},{8,12},{12,8},{16,20},{20,16},{24,28},{28,24},{1,5},{5... | collective-permute-start | bytes 491528 | tf_op jit(solution)/shard_map/ppermute | solution.py:491
  63.9 4.2 %copy-start.3 = (f32[5,8,8,128]{3,2,1,0:T(8,128)}, f32[5,8,8,128]{3,2,1,0:T(8,128)S(1)}, u32[]{:S(2)}) copy-start(f32[5,8,8,128]{3,2,1,0:T(8,128)S(1)} %collective-permute-done.9.refs_2_) | copy-start | bytes 491524
  63.9 4.1 %collective-permute-start.10 = (f32[5,8,8,128]{3,2,1,0:T(8,128)S(1)}, f32[5,8,8,128]{3,2,1,0:T(8,128)S(1)}, u32[]{:S(2)}, u32[]{:S(2)}) collective-permute-start(f32[5,8,8,128]{3,2,1,0:T(8,128)S(1)} %collective-permute-done.9.refs_2_), channel_id=1, source_target_pairs={{0,4},{4,0},{8,12},{12,8},{16,20},{20,16},{24,28},{28,24},{1,5},{5... | collective-permute-start | bytes 491528 | tf_op jit(solution)/shard_map/ppermute | solution.py:491
  64.3 3.8 %copy-start.16 = (f32[5,2,8,128]{3,2,1,0:T(8,128)}, f32[5,2,8,128]{3,2,1,0:T(8,128)S(1)}, u32[]{:S(2)}) copy-start(f32[5,2,8,128]{3,2,1,0:T(8,128)S(1)} %collective-permute-done.15.refs_9_) | copy-start | bytes 122884
  64.3 1.2 %collective-permute-start.21 = (f32[5,2,8,128]{3,2,1,0:T(8,128)S(1)}, f32[5,2,8,128]{3,2,1,0:T(8,128)S(1)}, u32[]{:S(2)}, u32[]{:S(2)}) collective-permute-start(f32[5,2,8,128]{3,2,1,0:T(8,128)S(1)} %collective-permute-done.20.refs_14_), channel_id=1, source_target_pairs={{0,4},{4,0},{8,12},{12,8},{16,20},{20,16},{24,28},{28,24},{1,5},{5... | collective-permute-start | bytes 122888 | tf_op jit(solution)/shard_map/ppermute | solution.py:491
  65.6 2.6 %copy-start.17 = (f32[5,2,8,128]{3,2,1,0:T(8,128)}, f32[5,2,8,128]{3,2,1,0:T(8,128)S(1)}, u32[]{:S(2)}) copy-start(f32[5,2,8,128]{3,2,1,0:T(8,128)S(1)} %collective-permute-done.21.refs_15_) | copy-start | bytes 122884
  65.6 1.2 %collective-permute-start.19 = (f32[5,2,8,128]{3,2,1,0:T(8,128)S(1)}, f32[5,2,8,128]{3,2,1,0:T(8,128)S(1)}, u32[]{:S(2)}, u32[]{:S(2)}) collective-permute-start(f32[5,2,8,128]{3,2,1,0:T(8,128)S(1)} %collective-permute-done.18.refs_12_), channel_id=1, source_target_pairs={{0,4},{4,0},{8,12},{12,8},{16,20},{20,16},{24,28},{28,24},{1,5},{5... | collective-permute-start | bytes 122888 | tf_op jit(solution)/shard_map/ppermute | solution.py:491
  66.8 1.4 %copy-start.18 = (f32[5,2,8,128]{3,2,1,0:T(8,128)}, f32[5,2,8,128]{3,2,1,0:T(8,128)S(1)}, u32[]{:S(2)}) copy-start(f32[5,2,8,128]{3,2,1,0:T(8,128)S(1)} %collective-permute-done.19.refs_13_) | copy-start | bytes 122884
  66.8 1.2 %collective-permute-start.17 = (f32[5,2,8,128]{3,2,1,0:T(8,128)S(1)}, f32[5,2,8,128]{3,2,1,0:T(8,128)S(1)}, u32[]{:S(2)}, u32[]{:S(2)}) collective-permute-start(f32[5,2,8,128]{3,2,1,0:T(8,128)S(1)} %collective-permute-done.16.refs_10_), channel_id=1, source_target_pairs={{0,4},{4,0},{8,12},{12,8},{16,20},{20,16},{24,28},{28,24},{1,5},{5... | collective-permute-start | bytes 122888 | tf_op jit(solution)/shard_map/ppermute | solution.py:491
  68.0 0.7 copy-start.4
  68.0 0.7 copy-start.5
  68.0 0.8 copy-start.6
  68.8 0.7 copy-start.7
  (1 other events, 0.6 us)
